TPU v7x, 32 devices: a whole 2x2x4 slice. The times are simulated.
32 devices in a mesh: node: 4 (over z), band: 8 (over y, x, core).
Axes of the slice: x: 2, y: 2, z: 4, core: 2. Of those that a mesh axis runs over, the one named last changes fastest.
Arguments:
- state0: float32 [2, 1024, 4, 3, 512], P(None, 'band'), may hold values from -36 to 36
- iterate: float32 [4, 2, 1024, 4, 3, 512], P('node', None, 'band'), may hold values from -37.2 to 37.2
- legendre: bfloat16 [1024, 512, 512], P('band'), may hold values from -0.25 to 0.25
- lat_weight: float32 [512], replicated, may hold values from 0.25 to 1
- coriolis: float32 [2, 512], replicated, may hold values from -1.5 to 1.5
- damping: float32 [1024, 3, 512], P('band'), may hold values from 0.1 to 10
- quadrature: float32 [4, 4], replicated, may hold values from 0.02 to 0.25
Outputs:
- updated: float32 [4, 2, 1024, 4, 3, 512], P('node', None, 'band')
- sweep_change: float32 [3], replicated
All inputs are finite; a program needn't handle non-finite values.
Results may differ from a plain program's by a relative error of at most 0.0017.
Values may be sent and summed in bfloat16 or wider, within the bound.
A program may use at most 256 MiB of HBM per device.

v0:
```python
import math

import jax
import jax.numpy as jnp
from jax import lax
from jax.sharding import PartitionSpec as P


def split_bf16(x):
    high = lax.reduce_precision(x, 8, 7)
    return high.astype(jnp.bfloat16), (x - high).astype(jnp.bfloat16)


def dft_table(parity, nband, local_modes, modes, points):
    fine = 32
    coarse = modes // fine
    column = lax.iota(jnp.int32, modes)
    pairs = local_modes // 2
    part = column // pairs % 2
    wave = column // local_modes * local_modes + column % pairs * 2 + parity
    unit = 2.0 * math.pi / points

    def angle(index):
        return (index % points).astype(jnp.float32) * unit

    big = angle(
        lax.iota(jnp.int32, coarse)[:, None] * fine * wave[None] + part[None] * (points // 4)
    )
    small = angle(lax.iota(jnp.int32, fine)[:, None] * wave[None])
    cos_big, sin_big = jnp.cos(big)[:, None], jnp.sin(big)[:, None]
    cos_small, sin_small = jnp.cos(small)[None], jnp.sin(small)[None]
    scale = 1.0 / math.sqrt(modes)
    slope_scale = wave.astype(jnp.float32) * (scale / modes)
    value = (cos_big * cos_small - sin_big * sin_small).reshape(modes, modes) * scale
    slope = -(sin_big * cos_small + cos_big * sin_small).reshape(modes, modes) * slope_scale
    return split_bf16(value), split_bf16(slope)


def mul(a, b, dims):
    return lax.dot_general(a, b, (dims, ((), ())), preferred_element_type=jnp.float32)


def body(state0, iterate, legendre, lat_weight, coriolis, damping, quadrature):
    spec = iterate[0]
    degrees = legendre.shape[2]
    half = degrees // 2
    local_modes, hemi = legendre.shape[:2]
    members, fields = spec.shape[2:4]
    nband = lax.axis_size("band")
    nnode = lax.axis_size("node")
    modes = local_modes * nband
    points = 2 * modes
    pairs = local_modes // 2
    lat_rows = hemi // nband
    node = lax.axis_index("node")
    band = lax.axis_index("band")
    tables = [dft_table(p, nband, local_modes, modes, points) for p in range(2)]
    cor = lax.dynamic_slice_in_dim(coriolis, band * lat_rows, lat_rows, 1)
    weight = lax.dynamic_slice_in_dim(lat_weight, band * lat_rows, lat_rows, 0)
    quad_row = lax.dynamic_slice_in_dim(quadrature, node, 1, 0)[0]
    diag = lax.dynamic_slice(quadrature, (node, node), (1, 1))[0, 0]
    is_even = lax.iota(jnp.int32, degrees) < half
    rate = damping[None, :, None]

    groups = 2
    ens = members // groups

    def synthesis(first):
        coeff = spec[:, :, first : first + ens].astype(jnp.bfloat16)
        coeff = coeff.transpose(1, 0, 3, 2, 4)
        zero = jnp.zeros((), jnp.bfloat16)
        rows = jnp.stack([jnp.where(is_even, coeff, zero), jnp.where(is_even, zero, coeff)], axis=1)
        rows = rows.reshape(local_modes, 4 * fields * ens, degrees)
        four = jnp.einsum("mrj,mlj->mrl", rows, legendre, preferred_element_type=jnp.float32)
        four = four.astype(jnp.bfloat16)
        four = four.reshape(pairs, 2, 2, 2, fields, ens, nband, lat_rows)
        four = four.transpose(6, 1, 3, 0, 2, 4, 5, 7)
        four = four.reshape(nband, 2, 2, pairs, 2 * fields * ens * lat_rows)
        return lax.all_to_all(four, "band", split_axis=0, concat_axis=0, tiled=True)

    def grid_step(four):
        shape = (modes, 2, fields, ens * lat_rows)
        parts = []
        for p in range(2):
            x = four[:, p].reshape(modes, -1)
            pair = []
            for high, low in tables[p]:
                dims = ((1,), (0,))
                pair.append((mul(high, x, dims) + mul(low, x, dims)).reshape(shape))
            parts.append(pair)
        tends = []
        for h in range(2):
            value, slope = (
                parts[0][v] + parts[1][v] if h == 0 else parts[0][v] - parts[1][v] for v in range(2)
            )
            hemis = []
            for s in range(2):
                val, slo = (
                    g[:, 0] + g[:, 1] if s == 0 else g[:, 0] - g[:, 1] for g in (value, slope)
                )
                c = jnp.tile(cor[s], ens)
                u, v, z = (val[:, f] for f in range(3))
                du, dv, dz = (slo[:, f] for f in range(3))
                hemis.append(
                    jnp.stack(
                        [-u * du + c * v - dz, -u * dv - c * u, -u * dz - (1.0 + z) * du], axis=1
                    )
                )
            tends.append(jnp.stack([hemis[0] + hemis[1], hemis[0] - hemis[1]], axis=1))
        scale = jnp.tile(weight, 2 * fields * ens)
        spectra = []
        for p in range(2):
            z = tends[0] + tends[1] if p == 0 else tends[0] - tends[1]
            zh, zl = split_bf16(z.reshape(modes, -1))
            high, low = tables[p][0]
            dims = ((0,), (0,))
            s = mul(high, zh, dims) + mul(high, zl, dims) + mul(low, zh, dims)
            spectra.append((s * scale).astype(jnp.bfloat16).reshape(nband, 2, pairs, -1))
        out = jnp.stack(spectra, axis=1)
        return lax.all_to_all(out, "band", split_axis=0, concat_axis=0, tiled=True)

    def analysis(out, first):
        out = out.reshape(nband, 2, 2, pairs, 2, fields, ens, lat_rows)
        out = out.transpose(3, 1, 4, 2, 5, 6, 0, 7)
        out = out.reshape(local_modes, 4 * fields * ens, hemi)
        both = jnp.einsum("mrl,mlj->mrj", out, legendre, preferred_element_type=jnp.float32)
        both = both.reshape(local_modes, 2, 2, fields, ens, degrees)
        nonlinear = jnp.where(is_even, both[:, 0], both[:, 1]).transpose(1, 0, 3, 2, 4)
        part = slice(first, first + ens)
        rest = nonlinear - rate * (spec[:, :, part] - state0[:, :, part])
        gathered = lax.all_gather(rest.astype(jnp.bfloat16), "node")
        mixed = sum(quad_row[p] * gathered[p].astype(jnp.float32) for p in range(nnode))
        return mixed

    received = [synthesis(g * ens) for g in range(groups)]
    spectra = [grid_step(r) for r in received]
    mixed = [analysis(s, g * ens) for g, s in enumerate(spectra)]
    mixed = jnp.concatenate(mixed, axis=2) - jnp.sum(quad_row) * (rate * state0)
    updated = (state0 + mixed + diag * rate * spec) / (1.0 + diag * rate)
    change = jnp.sum((updated - spec) ** 2, axis=(0, 1, 2, 4))
    base = jnp.sum(state0 * state0, axis=(0, 1, 2, 4))
    total = lax.psum(jnp.stack([change, base]), ("node", "band"))
    ratio = jnp.sqrt(total[0] / (total[1] + 1e-06))
    return (updated[None], ratio)


def solution(mesh):
    placed = (
        P(None, "band", None, None, None),
        P("node", None, "band", None, None, None),
        P("band", None, None),
        P(),
        P(),
        P("band", None, None),
        P(),
    )
    return jax.shard_map(
        body,
        mesh=mesh,
        in_specs=placed,
        out_specs=(P("node", None, "band", None, None, None), P()),
        check_vma=False,
    )
```

profile of v0, /device:TPU:0, one launch (start us, length us, event | category | flops | bytes accessed | tf_op | source)
XLA Modules:
  0.0 769.7 jit_solution(12251660246669993909)
XLA Ops:
  25.5 27.3 %convolution_convert_fusion = bf16[128,24,512]{2,1,0:T(8,128)(2,1)} fusion(bf16[128,24,512]{2,1,0:T(8,128)(2,1)S(1)} %reshape.1694, bf16[128,512,512]{2,1,0:T(8,128)(2,1)} %param.9), kind=kOutput, calls=%fused_computation.75 | convolution fusion | flops 1612185600 | bytes 73400320 | tf_op jit(solution)/shard_map/mrj,mlj->mrl/dot_general | solution.py:74
  52.8 8.9 %reshape.1695 = bf16[64,2,2,2,3,2,8,64]{7,6,5,4,3,2,1,0:T(8,128)(2,1)} reshape(bf16[128,24,512]{2,1,0:T(8,128)(2,1)} %convolution_convert_fusion) | data formatting | bytes 6291456 | tf_op jit(solution)/shard_map/reshape | solution.py:76
  61.7 10.4 %copy.92 = bf16[64,2,2,2,3,2,8,64]{7,5,4,2,0,3,1,6:T(2,128)(2,1)} copy(bf16[64,2,2,2,3,2,8,64]{7,6,5,4,3,2,1,0:T(8,128)(2,1)} %reshape.1695) | data formatting | bytes 6291456 | tf_op jit(solution)/shard_map/reshape | solution.py:76
  72.0 12.2 %reshape.1696 = bf16[8,2,2,64,768]{4,3,2,1,0:T(8,128)(2,1)} reshape(bf16[8,2,2,64,2,3,2,64]{7,6,5,4,3,2,1,0:T(2,128)(2,1)} %bitcast.278) | data formatting | bytes 6291456 | tf_op jit(solution)/shard_map/reshape | solution.py:78
  99.7 27.3 %convolution_convert_fusion.1 = bf16[128,24,512]{2,1,0:T(8,128)(2,1)} fusion(bf16[128,24,512]{2,1,0:T(8,128)(2,1)S(1)} %reshape.1688, bf16[128,512,512]{2,1,0:T(8,128)(2,1)} %param.9), kind=kOutput, calls=%fused_computation.76 | convolution fusion | flops 1612185600 | bytes 73400320 | tf_op jit(solution)/shard_map/mrj,mlj->mrl/dot_general | solution.py:74
  127.0 8.9 %reshape.1689 = bf16[64,2,2,2,3,2,8,64]{7,6,5,4,3,2,1,0:T(8,128)(2,1)} reshape(bf16[128,24,512]{2,1,0:T(8,128)(2,1)} %convolution_convert_fusion.1) | data formatting | bytes 6291456 | tf_op jit(solution)/shard_map/reshape | solution.py:76
  135.9 10.4 %copy.94 = bf16[64,2,2,2,3,2,8,64]{7,5,4,2,0,3,1,6:T(2,128)(2,1)} copy(bf16[64,2,2,2,3,2,8,64]{7,6,5,4,3,2,1,0:T(8,128)(2,1)} %reshape.1689) | data formatting | bytes 6291456 | tf_op jit(solution)/shard_map/reshape | solution.py:76
  146.2 12.2 %reshape.1690 = bf16[8,2,2,64,768]{4,3,2,1,0:T(8,128)(2,1)} reshape(bf16[8,2,2,64,2,3,2,64]{7,6,5,4,3,2,1,0:T(2,128)(2,1)} %bitcast.279) | data formatting | bytes 6291456 | tf_op jit(solution)/shard_map/reshape | solution.py:78
  172.7 8.2 %fusion.5 = (bf16[32,32,1024]{2,1,0:T(8,128)(2,1)}, bf16[32,32,1024]{2,1,0:T(8,128)(2,1)}, bf16[32,32,1024]{2,1,0:T(8,128)(2,1)S(1)}, bf16[32,32,1024]{2,1,0:T(8...) fusion(f32[1024]{0:T(1024)S(1)} %convert_multiply_fusion.1, ...), kind=kLoop, calls=%fused_computation.29 | loop fusion | flops 35651584 | bytes 17833984 | tf_op jit(solution)/shard_map/convert_element_type | solution.py:11
  192.9 15.6 %all-to-all-done = bf16[8,2,2,64,768]{4,3,2,1,0:T(8,128)(2,1)} async-done(((bf16[8,2,2,64,768]{4,3,2,1,0:T(8,128)(2,1)}), bf16[8,2,2,64,768]{4,3,2,1,0:T(8,128)(2,1)}, u32[]{:S(2)}, u32[]{:S(2)}) %all-to-all-start) | async-done | bytes 3145760 | tf_op jit(solution)/shard_map/all_to_all | solution.py:79
  307.0 12.2 %reshape.1697 = bf16[8,2,2,64,2,3,2,64]{7,6,5,4,3,2,1,0:T(2,128)(2,1)} reshape(bf16[8,2,2,64,768]{4,3,2,1,0:T(8,128)(2,1)} %all-to-all-done.3) | data formatting | bytes 6291456 | tf_op jit(solution)/shard_map/reshape | solution.py:123
  319.3 12.7 %copy.91 = bf16[8,2,2,64,2,3,2,64]{7,0,6,5,2,4,1,3:T(8,128)(2,1)} copy(bf16[8,2,2,64,2,3,2,64]{7,6,5,4,3,2,1,0:T(2,128)(2,1)} %reshape.1697) | data formatting | bytes 6291456 | tf_op jit(solution)/shard_map/reshape | solution.py:123
  331.9 8.0 %reshape.1698 = bf16[128,24,512]{2,1,0:T(8,128)(2,1)S(1)} reshape(bf16[64,2,2,2,3,2,8,64]{7,6,5,4,3,2,1,0:T(8,128)(2,1)} %bitcast.280) | data formatting | bytes 6291456 | tf_op jit(solution)/shard_map/reshape | solution.py:125
  340.0 25.5 %fusion.165 = f32[128,24,512]{2,1,0:T(8,128)} fusion(bf16[128,24,512]{2,1,0:T(8,128)(2,1)S(1)} %reshape.1698, bf16[128,512,512]{2,1,0:T(8,128)(2,1)} %param.9), kind=kOutput, calls=%fused_computation.319 | convolution fusion | flops 1610612736 | bytes 76546048 | tf_op jit(solution)/shard_map/mrl,mlj->mrj/dot_general | solution.py:126
  365.5 8.2 %reshape.1699 = f32[128,2,2,3,2,512]{5,4,3,2,1,0:T(2,128)} reshape(f32[128,24,512]{2,1,0:T(8,128)} %fusion.165) | data formatting | bytes 12582912 | tf_op jit(solution)/shard_map/reshape | solution.py:127
  381.5 12.0 %reshape.1691 = bf16[8,2,2,64,2,3,2,64]{7,6,5,4,3,2,1,0:T(2,128)(2,1)} reshape(bf16[8,2,2,64,768]{4,3,2,1,0:T(8,128)(2,1)} %all-to-all-done.1) | data formatting | bytes 6291456 | tf_op jit(solution)/shard_map/reshape | solution.py:123
  393.5 12.7 %copy.93 = bf16[8,2,2,64,2,3,2,64]{7,0,6,5,2,4,1,3:T(8,128)(2,1)} copy(bf16[8,2,2,64,2,3,2,64]{7,6,5,4,3,2,1,0:T(2,128)(2,1)} %reshape.1691) | data formatting | bytes 6291456 | tf_op jit(solution)/shard_map/reshape | solution.py:123
  414.1 25.5 %fusion.156 = f32[128,24,512]{2,1,0:T(8,128)} fusion(bf16[128,24,512]{2,1,0:T(8,128)(2,1)S(1)} %reshape.1692, bf16[128,512,512]{2,1,0:T(8,128)(2,1)} %param.9), kind=kOutput, calls=%fused_computation.310 | convolution fusion | flops 1610612736 | bytes 76546048 | tf_op jit(solution)/shard_map/mrl,mlj->mrj/dot_general | solution.py:126
  439.7 8.6 %reshape.1693 = f32[128,2,2,3,2,512]{5,4,3,2,1,0:T(2,128)} reshape(f32[128,24,512]{2,1,0:T(8,128)} %fusion.156) | data formatting | bytes 12582912 | tf_op jit(solution)/shard_map/reshape | solution.py:127
  455.2 8.3 %fusion.16 = (bf16[2,128,2,3,512]{4,1,3,2,0:T(8,128)(2,1)}, bf16[2,128,2,3,512]{4,1,3,2,0:T(8,128)(2,1)}) fusion(f32[2,128,4,3,512]{4,1,3,2,0:T(8,128)} %copy.53, f32[128,1,2,3,2,512]{5,4,3,2,1,0:T(2,128)} %get-tuple-element.17, f32[128,1,2,3,2,512]{5,4,3,2,1,0:T(2,128)S(1)} %get-tuple-element.16, f32[2,128,4,3,512]{4,1,3,2,0:T(8,128)S(1)} %bitcast.277, ...), kind=kLoop, calls=%fused_computation.46 | loop fusion | flops 7864320 | bytes 29098496 | tf_op jit(solution)/shard_map/convert_element_type | solution.py:131
  472.5 108.7 %all-gather.5.cloned.1.call-done = bf16[8,128,2,3,512]{4,1,3,2,0:T(8,128)(2,1)} async-done(((bf16[2,128,2,3,512]{4,1,3,2,0:T(8,128)(2,1)}), bf16[8,128,2,3,512]{4,1,3,2,0:T(8,128)(2,1)}) %all-gather.5.cloned.1.call-update) | async-done | bytes 6291472 | tf_op jit(solution)/shard_map/all_gather | solution.py:131
  587.9 108.5 %all-gather.7.cloned.1.call-done = bf16[8,128,2,3,512]{4,1,3,2,0:T(8,128)(2,1)} async-done(((bf16[2,128,2,3,512]{4,1,3,2,0:T(8,128)(2,1)}), bf16[8,128,2,3,512]{4,1,3,2,0:T(8,128)(2,1)}) %all-gather.7.cloned.1.call-update) | async-done | bytes 6291472 | tf_op jit(solution)/shard_map/all_gather | solution.py:131
  703.2 13.6 %multiply_reduce_fusion.1 = (f32[3]{0:T(128)S(1)}, f32[2,128,4,3,512]{4,1,3,2,0:T(8,128)S(1)}) fusion(f32[1,2,128,4,3,512]{5,3,4,2,1,0:T(4,128)} %param.8, f32[128,3,512]{2,0,1:T(8,128)S(1)} %copy-done.13, f32[128,3,512]{2,0,1:T(8,128)S(1)} %copy-done.14, f32[128,3,512]{2,0,1:T(8,128)S(1)} %copy-done.12, f32[]{:T(128)} %get-tuple-element.6, ...), kind=kLoop, calls=%fused_computation.10 | loop fusion | flops 17301500 | bytes 27525136 | tf_op jit(solution)/shard_map/reduce_sum | solution.py:140
  723.5 38.3 %psum.7 = f32[2,3]{1,0:T(2,128)S(1)} all-reduce(f32[2,3]{1,0:T(2,128)S(1)} %pad_maximum_fusion.16), channel_id=1, replica_groups=mesh['node'=4,'band'=8] {'node','band'}, use_global_device_ids=true, to_apply=%region_3.4 | all-reduce | flops 6 | bytes 48 | tf_op jit(solution)/shard_map/psum | solution.py:142
  (184 shorter events, 210.1 us)
Async XLA Ops:
  7.2 82.5 %copy-start = (f32[2,512]{1,0:T(2,128)S(1)}, f32[2,512]{1,0:T(2,128)}, u32[]{:S(2)}) copy-start(f32[2,512]{1,0:T(2,128)} %param.11) | copy-start | bytes 12292
  84.2 6.6 copy-start.8
  84.2 81.6 %all-to-all-start.2 = ((bf16[8,2,2,64,768]{4,3,2,1,0:T(8,128)(2,1)}), bf16[8,2,2,64,768]{4,3,2,1,0:T(8,128)(2,1)}, u32[]{:S(2)}, u32[]{:S(2)}) async-start(bf16[8,2,2,64,768]{4,3,2,1,0:T(8,128)(2,1)} %reshape.1696), calls=%async_computation.2 | async-start | bytes 6291456 | tf_op jit(solution)/shard_map/all_to_all | solution.py:79
  165.8 42.7 %all-to-all-start = ((bf16[8,2,2,64,768]{4,3,2,1,0:T(8,128)(2,1)}), bf16[8,2,2,64,768]{4,3,2,1,0:T(8,128)(2,1)}, u32[]{:S(2)}, u32[]{:S(2)}) async-start(bf16[8,2,2,64,768]{4,3,2,1,0:T(8,128)(2,1)} %reshape.1690), calls=%async_computation | async-start | bytes 6291456 | tf_op jit(solution)/shard_map/all_to_all | solution.py:79
  181.0 4.8 copy-start.26
  181.0 8.4 %copy-start.19 = (bf16[32,32,1024]{2,1,0:T(8,128)(2,1)}, bf16[32,32,1024]{2,1,0:T(8,128)(2,1)S(1)}, u32[]{:S(2)}) copy-start(bf16[32,32,1024]{2,1,0:T(8,128)(2,1)S(1)} %get-tuple-element.116) | copy-start | bytes 6291460
  210.8 15.3 %copy-start.5 = (bf16[8,1,2,64,768]{4,3,2,1,0:T(8,128)(2,1)}, bf16[8,1,2,64,768]{4,3,2,1,0:T(8,128)(2,1)S(1)}, u32[]{:S(2)}) copy-start(bf16[8,1,2,64,768]{4,3,2,1,0:T(8,128)(2,1)S(1)} %get-tuple-element.69) | copy-start | bytes 4718596
  259.8 42.7 %all-to-all-start.3 = ((bf16[8,2,2,64,768]{4,3,2,1,0:T(8,128)(2,1)}), bf16[8,2,2,64,768]{4,3,2,1,0:T(8,128)(2,1)}, u32[]{:S(2)}, u32[]{:S(2)}) async-start(bf16[8,2,2,64,768]{4,3,2,1,0:T(8,128)(2,1)} %pad_maximum_fusion.7), calls=%async_computation.3 | async-start | bytes 6291456 | tf_op jit(solution)/shard_map/all_to_all | solution.py:120
  264.6 5.2 copy-start.4
  264.6 5.2 copy-start.6
  264.6 5.2 copy-start.16
  302.5 79.0 %all-to-all-start.1 = ((bf16[8,2,2,64,768]{4,3,2,1,0:T(8,128)(2,1)}), bf16[8,2,2,64,768]{4,3,2,1,0:T(8,128)(2,1)}, u32[]{:S(2)}, u32[]{:S(2)}) async-start(bf16[8,2,2,64,768]{4,3,2,1,0:T(8,128)(2,1)} %pad_maximum_fusion.3), calls=%async_computation.1 | async-start | bytes 6291456 | tf_op jit(solution)/shard_map/all_to_all | solution.py:120
  307.0 274.3 %all-gather.5.cloned.1.call-start = ((), (), s32[]{:S(2)}) async-start(), calls=%async_computation.4 | async-start | bytes 7864320 | tf_op jit(solution)/shard_map/all_gather | solution.py:131
  439.7 15.4 %slice-start = ((s8[6291456]{0:T(1024)(128)(4,1)}), s8[2097152]{0:T(1024)(128)(4,1)S(1)}, s32[]{:S(2)}) async-start(s8[6291456]{0:T(1024)(128)(4,1)} %bitcast.275), calls=%async_computation.6 | async-start | bytes 4194304
  448.3 6.9 slice-start.1
  448.3 6.8 copy-start.9
  448.3 6.8 copy-start.10
  448.3 6.8 copy-start.11
  448.3 6.8 copy-start.33
  463.5 232.9 %all-gather.7.cloned.1.call-start = ((), (), s32[]{:S(2)}) async-start(), calls=%async_computation.5 | async-start | bytes 7864320 | tf_op jit(solution)/shard_map/all_gather | solution.py:131
  696.4 6.7 copy-start.12
  696.4 6.8 copy-start.13
  696.4 6.8 copy-start.14
  716.8 45.6 %copy-start.1 = (f32[2,512]{1,0:T(2,128)S(1)}, f32[2,512]{1,0:T(2,128)}, u32[]{:S(2)}) copy-start(f32[2,512]{1,0:T(2,128)} %param.11) | copy-start | bytes 12292
  (22 other events, 59.8 us)
Sparse Core Ops, SparseCore 0:
  463.6 117.6 all-gather.4
  582.8 113.5 all-gather.6
where the time goes:
time: 781 us; the launch traced here: 770 us
  waiting for transfers between devices  239 us (31%)
  local copies, waits for them, and re-layouts  212 us (27%)
  matrix products  173 us (22%)
  other arithmetic  72.5 us (9%)
  blocking collectives  38.3 us (5%)
  starting transfers between devices  19.7 us (3%)
  between operations  15.3 us (2%)
    all_gather x2, waiting for transfers between devices, analysis(): gathered = lax.all_gather(rest.astype(jnp.bfloat16), 'node')  217 us
    dot_general x28, matrix products, mul(): lax.dot_general(a, b, (dims, ((), ())), preferred_element_type=jnp.float32)  67.6 us
    dot_general x2, matrix products, synthesis(): jnp.einsum('mrj,mlj->mrl', rows, legendre, preferred_element_type=jnp.flo...  54.6 us
    dot_general x2, matrix products, analysis(): jnp.einsum('mrl,mlj->mrj', out, legendre, preferred_element_type=jnp.floa...  51.1 us
    reshape x4, local copies, waits for them, and re-layouts, analysis(): out = out.reshape(nband, 2, 2, pairs, 2, fields, ens, lat_rows)  49.5 us
    reshape x4, local copies, waits for them, and re-layouts, synthesis(): four = four.reshape(pairs, 2, 2, 2, fields, ens, nband, lat_rows)  38.5 us
    psum x1, blocking collectives, body(): total = lax.psum(jnp.stack([change, base]), ('node', 'band'))  38.3 us
    unnamed x83, local copies, waits for them, and re-layouts  24.9 us
  transfers between devices with their start and end apart: 6, of which 4 were waited for; matrix products, arithmetic and copies ran while one was open for 28% of the time, Pallas kernels for 0%

commit v1 on v0

--- a/solution.py
+++ b/solution.py
@@ -1,9 +1,19 @@
+import functools
 import math
 
 import jax
 import jax.numpy as jnp
+import numpy as np
 from jax import lax
+from jax.experimental import pallas as pl
+from jax.experimental.pallas import tpu as pltpu
 from jax.sharding import PartitionSpec as P
+
+MESH = pl.DeviceIdType.MESH
+F32, BF16 = jnp.float32, jnp.bfloat16
+VMEM_BYTES = 63_000_000
+LANES = 128
+SUB = 4
 
 
 def split_bf16(x):
@@ -40,7 +50,7 @@
     return lax.dot_general(a, b, (dims, ((), ())), preferred_element_type=jnp.float32)
 
 
-def body(state0, iterate, legendre, lat_weight, coriolis, damping, quadrature):
+def plain_body(state0, iterate, legendre, lat_weight, coriolis, damping, quadrature):
     spec = iterate[0]
     degrees = legendre.shape[2]
     half = degrees // 2
@@ -144,6 +154,743 @@
     return (updated[None], ratio)
 
 
+class Plan:
+    def __init__(self, nband, nnode, iterate, legendre):
+        self.n, self.nnode = nband, nnode
+        self.modes, self.members, self.fields, self.degrees = iterate[2:]
+        self.hemi = legendre[1]
+        self.ml = self.modes // nband
+        self.lb = LANES
+        self.nlb = self.hemi // self.lb
+        self.eg = max(nband // max(self.nlb, 1), 1)
+        self.el = self.members // self.eg
+        self.rows = 2 * self.members * self.fields
+        self.pl = self.ml // 2
+        self.mc = 32
+        self.nc = self.ml // self.mc
+        self.half = self.modes // 2
+        self.kc = (self.half + 16) // 3
+        self.g = 4 * self.fields
+        self.fits = (
+            nnode == 4
+            and self.fields == 3
+            and self.nlb * self.eg == nband
+            and self.eg * self.el == self.members
+            and self.hemi % self.lb == 0
+            and self.ml % self.mc == 0
+            and self.modes % nband == 0
+            and (self.half + 16) % 48 == 0
+            and self.rows % 8 == 0
+            and self.degrees % 256 == 0
+        )
+
+
+def greet(axis, peers):
+    sem = pltpu.get_barrier_semaphore()
+    for peer in peers:
+        pl.semaphore_signal(sem, inc=1, device_id={axis: peer}, device_id_type=MESH)
+    pl.semaphore_wait(sem, len(peers))
+
+
+def gather_rows(d, rows, piece):
+    for cc in range(2):
+        for e in range(d.members):
+            r = (cc * d.members + e) * d.fields
+            rows[r : r + d.fields, :] = piece(cc, e)
+
+
+def build_tables(d, trig, fwd, back):
+    tall, fine = 3 * d.kc // 16, 16
+    short = d.half // 16
+
+    def turn(big, small):
+        cb, sb, cs, ss = trig[0, big], trig[1, big], trig[0, small], trig[1, small]
+        return cb * cs - sb * ss, -(sb * cs + cb * ss)
+
+    for p in range(2):
+        ramp = (2 * lax.broadcasted_iota(jnp.int32, (1, d.half), 1) + p).astype(F32) * (1.0 / d.modes)
+
+        def ahead(a, _):
+            cos, sin = turn(pl.ds(p * tall + a, 1), pl.ds((2 * tall + short + p * fine), fine))
+            inside = lax.broadcasted_iota(jnp.int32, (fine, 1), 0) + a * fine <= d.half
+            cos, sin = jnp.where(inside, cos, 0.0), jnp.where(inside, sin, 0.0)
+            c = a // (d.kc // 16)
+            at = (a - c * (d.kc // 16)) * 16
+            for cc, pair in enumerate(((cos, ramp * sin), (sin, -ramp * cos))):
+                for v, t in enumerate(pair):
+                    top = t.astype(BF16)
+                    fwd[p, cc, c, pl.ds(pl.multiple_of(2 * v * d.kc + at, 16), 16)] = top
+                    fwd[p, cc, c, pl.ds(pl.multiple_of((2 * v + 1) * d.kc + at, 16), 16)] = (
+                        t - top.astype(F32)
+                    ).astype(BF16)
+            return _
+
+        lax.fori_loop(0, tall, ahead, None)
+        first = jnp.where(lax.broadcasted_iota(jnp.int32, (1, d.half), 1) == 0, 0.5, 1.0)
+
+        def behind(a, _):
+            pair = turn(pl.ds(2 * tall + a, 1), pl.ds(2 * tall + short + (2 + p) * fine, fine))
+            for cc, t in enumerate(pair):
+                t = t * first
+                top = t.astype(BF16)
+                at = pl.multiple_of(a * 16, 16)
+                back[p, cc, pl.ds(at, 16)] = top
+                back[p, cc, pl.ds(pl.multiple_of(d.half + at, 16), 16)] = (t - top.astype(F32)).astype(BF16)
+            return _
+
+        lax.fori_loop(0, short, behind, None)
+
+
+def trig_rows(d):
+    points = 2 * d.modes
+    tall, short = 3 * d.kc // 16, d.half // 16
+    wave = 2 * np.arange(d.half)
+    k = np.arange(d.half)
+    big = [16 * np.arange(tall)[:, None] * (wave + p)[None] for p in range(2)]
+    big.append(32 * np.arange(short)[:, None] * k[None])
+    small = [np.arange(16)[:, None] * (wave + p)[None] for p in range(2)]
+    small += [(2 * np.arange(16) + p)[:, None] * k[None] for p in range(2)]
+    angle = np.concatenate(big + small) % points * (2.0 * np.pi / points)
+    scale = np.where(np.arange(len(angle)) < 2 * tall + short, d.modes**-0.5, 1.0)[:, None]
+    return np.stack([np.cos(angle) * scale, np.sin(angle) * scale]).astype(np.float32)
+
+
+def synthesis_kernel(
+    d, it_hbm, leg_hbm, trig, out, fwd_hbm, back_hbm, raw, rows, leg, stage, send, fwd, back,
+    leg_sem, send_sem, recv_sem, own_sem, tab_sem,
+):
+    me = lax.axis_index("band")
+    n, half, per = d.n, d.degrees // 2, d.mc // 2
+    subs = d.mc // SUB
+    peers = [lax.rem(me + off, n) for off in range(1, n)]
+    greet("band", peers)
+
+    def fetch(i, slot):
+        return [
+            pltpu.make_async_copy(leg_hbm.at[pl.ds(i * SUB, SUB)], leg.at[slot], leg_sem.at[slot, 0]),
+            pltpu.make_async_copy(it_hbm.at[0, :, pl.ds(i * SUB, SUB)], raw.at[slot], leg_sem.at[slot, 1]),
+        ]
+
+    def remote(c, off):
+        peer = lax.rem(me + off, n)
+        return pltpu.make_async_remote_copy(
+            src_ref=send.at[c, peer],
+            dst_ref=out.at[:, me, pl.ds(c * per, per)],
+            send_sem=send_sem.at[c, off],
+            recv_sem=recv_sem.at[c, off],
+            device_id={"band": peer},
+            device_id_type=MESH,
+        )
+
+    def local(c):
+        return pltpu.make_async_copy(
+            send.at[c, me], out.at[:, me, pl.ds(c * per, per)], own_sem.at[c]
+        )
+
+    for copy_in in fetch(0, 0):
+        copy_in.start()
+
+    def chunk(c, _):
+        def sub(j, _):
+            i = c * subs + j
+            slot = lax.rem(i, 2)
+
+            @pl.when(i + 1 < d.nc * subs)
+            def _():
+                for copy_in in fetch(i + 1, 1 - slot):
+                    copy_in.start()
+
+            for copy_in in fetch(i, slot):
+                copy_in.wait()
+            for mi in range(SUB):
+                gather_rows(d, rows.at[mi], lambda cc, e: raw[slot, cc, mi, e])
+            for mi in range(SUB):
+                x = rows[mi].astype(BF16)
+                table = leg[slot, mi]
+                for par in range(2):
+                    cols = slice(par * half, (par + 1) * half)
+                    y = mul(x[:, cols], table[:, cols], ((1,), (1,)))
+                    for lb in range(d.nlb):
+                        at = (lb * 2 + par) * d.rows * d.mc + (mi % 2) * per + j * (SUB // 2) + mi // 2
+                        stage[pl.ds(at, d.rows, stride=d.mc), :] = y[:, lb * LANES : (lb + 1) * LANES]
+            return _
+
+        lax.fori_loop(0, subs, sub, None)
+        for s in range(d.el):
+            for f in range(d.fields):
+                for p in range(2):
+                    for cc in range(2):
+                        g = ((s * d.fields + f) * 2 + p) * 2 + cc
+                        for lb in range(d.nlb):
+                            for eg in range(d.eg):
+                                r = (cc * d.members + eg * d.el + s) * d.fields + f
+                                tiles = [
+                                    stage[pl.ds(((lb * 2 + par) * d.rows + r) * d.mc + p * per, per), :]
+                                    for par in range(2)
+                                ]
+                                send[c, lb * d.eg + eg, g] = jnp.concatenate(tiles, axis=1).astype(BF16)
+        for off in range(1, n):
+            remote(c, off).start()
+        local(c).start()
+        return _
+
+    lax.fori_loop(0, d.nc, chunk, None)
+    build_tables(d, trig, fwd, back)
+    saves = [
+        pltpu.make_async_copy(fwd, fwd_hbm, tab_sem.at[0]),
+        pltpu.make_async_copy(back, back_hbm, tab_sem.at[1]),
+    ]
+    for save in saves:
+        save.start()
+
+    def finish(c, _):
+        for off in range(1, n):
+            remote(c, off).wait()
+        local(c).wait()
+        return _
+
+    lax.fori_loop(0, d.nc, finish, None)
+    for save in saves:
+        save.wait()
+
+
+def synthesis(d, iterate, legendre, trig):
+    blocks = d.el * d.g
+    fwd = (2, 2, 3, 4 * d.kc, d.half)
+    back = (2, 2, 2 * d.half, d.half)
+    anywhere = pl.BlockSpec(memory_space=pl.ANY)
+    return pl.pallas_call(
+        functools.partial(synthesis_kernel, d),
+        name="synthesis",
+        out_shape=(
+            jax.ShapeDtypeStruct((blocks, d.n, d.pl, 2 * d.lb), BF16),
+            jax.ShapeDtypeStruct(fwd, BF16),
+            jax.ShapeDtypeStruct(back, BF16),
+        ),
+        in_specs=[anywhere, anywhere, pl.BlockSpec(memory_space=pltpu.VMEM)],
+        out_specs=(anywhere,) * 3,
+        scratch_shapes=[
+            pltpu.VMEM((2, 2, SUB, d.members, d.fields, d.degrees), F32),
+            pltpu.VMEM((SUB, d.rows, d.degrees), F32),
+            pltpu.VMEM((2, SUB, d.hemi, d.degrees), BF16),
+            pltpu.VMEM((2 * d.nlb * d.rows * d.mc, LANES), F32),
+            pltpu.VMEM((d.nc, d.n, blocks, d.mc // 2, 2 * d.lb), BF16),
+            pltpu.VMEM(fwd, BF16),
+            pltpu.VMEM(back, BF16),
+            pltpu.SemaphoreType.DMA((2, 2)),
+            pltpu.SemaphoreType.DMA((d.nc, d.n)),
+            pltpu.SemaphoreType.DMA((d.nc, d.n)),
+            pltpu.SemaphoreType.DMA((d.nc,)),
+            pltpu.SemaphoreType.DMA((2,)),
+        ],
+        compiler_params=pltpu.CompilerParams(
+            collective_id=1, has_side_effects=True, vmem_limit_bytes=VMEM_BYTES
+        ),
+    )(iterate, legendre, trig)
+
+
+def four_points(ce, se, co, so):
+    a, b, c, e = ce + se, ce - se, co + so, co - so
+    return a + c, b + e, a - c, b - e
+
+
+def fold_points(t):
+    s13, s24, d13, d24 = t[0] + t[2], t[1] + t[3], t[0] - t[2], t[1] - t[3]
+    return s13 + s24, s13 - s24, d13 + d24, d13 - d24
+
+
+def grid_kernel(
+    d, x_hbm, fwd_hbm, back_hbm, cor, weight, out, x, fwd, back, part, high, low, edge, send,
+    x_sem, tab_sem, send_sem, recv_sem, own_sem,
+):
+    me = lax.axis_index("band")
+    n, kc, lb, g = d.n, d.kc, d.lb, d.g
+    peers = [lax.rem(me + off, n) for off in range(1, n)]
+
+    def fetch(s):
+        return pltpu.make_async_copy(x_hbm.at[pl.ds(s * g, g)], x.at[lax.rem(s, 2)], x_sem.at[lax.rem(s, 2)])
+
+    tables = [
+        pltpu.make_async_copy(fwd_hbm, fwd, tab_sem.at[0]),
+        pltpu.make_async_copy(back_hbm, back, tab_sem.at[1]),
+    ]
+    fetch(0).start()
+    for t in tables:
+        t.start()
+    greet("band", peers)
+
+    def remote(s, f, off):
+        peer = lax.rem(me + off, n)
+        return pltpu.make_async_remote_copy(
+            src_ref=send.at[pl.ds(s * g + f * 4, 4), pl.ds(peer * d.pl, d.pl)],
+            dst_ref=out.at[s, me, pl.ds(f * 4, 4)],
+            send_sem=send_sem.at[s * d.fields + f, off],
+            recv_sem=recv_sem.at[s * d.fields + f, off],
+            device_id={"band": peer},
+            device_id_type=MESH,
+        )
+
+    def local(s, f):
+        return pltpu.make_async_copy(
+            send.at[pl.ds(s * g + f * 4, 4), pl.ds(me * d.pl, d.pl)],
+            out.at[s, me, pl.ds(f * 4, 4)],
+            own_sem.at[s * d.fields + f],
+        )
+
+    for t in tables:
+        t.wait()
+
+    def step(s, _):
+        slot = lax.rem(s, 2)
+
+        @pl.when(s + 1 < d.el)
+        def _():
+            fetch(s + 1).start()
+
+        fetch(s).wait()
+
+        def rows(c, _):
+            def field(f, _):
+                for p in range(2):
+                    for cc in range(2):
+                        q = p * 2 + cc
+                        part[f * 4 + q] = mul(fwd[p, cc, c], x[slot, f * 4 + q], ((1,), (0,)))
+                return _
+
+            lax.fori_loop(0, d.fields, field, None)
+
+            def block(i, _):
+                def load(f, q, v):
+                    return part[f * 4 + q, pl.ds(2 * v * kc + i * 16, 16)] + part[
+                        f * 4 + q, pl.ds((2 * v + 1) * kc + i * 16, 16)
+                    ]
+
+                folded = []
+                comps = [[[load(f, q, v) for q in range(4)] for v in range(2)] for f in range(d.fields)]
+                for h in range(2):
+                    val, slo = [], []
+                    for f in range(d.fields):
+                        hemi = [
+                            [a[:, :lb] + a[:, lb:] if h == 0 else a[:, :lb] - a[:, lb:] for a in comps[f][v]]
+                            for v in range(2)
+                        ]
+                        val.append(four_points(*hemi[0]))
+                        g0, g1, g2, g3 = hemi[1]
+                        slo.append(four_points(g1, g0, g3, g2))
+                    c_lat = cor[h : h + 1]
+                    tend = [[], [], []]
+                    for k in range(4):
+                        u, w, z = (val[f][k] for f in range(3))
+                        du, dw, dz = (slo[f][k] for f in range(3))
+                        tend[0].append(c_lat * w - u * du - dz)
+                        tend[1].append(-u * dw - c_lat * u)
+                        tend[2].append(-u * dz - (1.0 + z) * du)
+                    folded.append([fold_points(t) for t in tend])
+                at = pl.multiple_of(c * kc + i * 16, 16)
+                for f in range(d.fields):
+                    for q in range(4):
+                        north, south = folded[0][f][q], folded[1][f][q]
+                        t = jnp.concatenate([north + south, north - south], axis=1)
+                        top = t.astype(BF16)
+                        high[f * 4 + q, pl.ds(at, 16)] = top
+                        low[f * 4 + q, pl.ds(at, 16)] = (t - top.astype(F32)).astype(BF16)
+                        edge[f * 4 + q] = t[:8]
+                return _
+
+            lax.fori_loop(0, kc // 16, block, None)
+            return _
+
+        lax.fori_loop(0, 3, rows, None)
+
+        def field(f, _):
+            for q in range(4):
+                p, cc = divmod(q, 2)
+                both = mul(back[p, cc], high[f * 4 + q, : d.half], ((1,), (0,)))
+                spec = both[: d.half] + both[d.half :]
+                spec = spec + mul(back[p, cc, : d.half], low[f * 4 + q, : d.half], ((1,), (0,)))
+                if p == cc:
+                    sign = 1.0 - 2.0 * (lax.broadcasted_iota(jnp.int32, (d.half, 1), 0) % 2).astype(F32)
+                    scale = 0.5 / math.sqrt(d.modes) * (1.0 if p == 0 else -1.0)
+                    spec = spec + (sign * scale) * edge[f * 4 + q, :1]
+                send[s * g + f * 4 + q] = (spec * weight[...]).astype(BF16)
+            for off in range(1, n):
+                remote(s, f, off).start()
+            local(s, f).start()
+            return _
+
+        lax.fori_loop(0, d.fields, field, None)
+        return _
+
+    lax.fori_loop(0, d.el, step, None)
+
+    def finish(i, _):
+        s, f = i // d.fields, i % d.fields
+        for off in range(1, n):
+            remote(s, f, off).wait()
+        local(s, f).wait()
+        return _
+
+    lax.fori_loop(0, d.el * d.fields, finish, None)
+
+
+def grid_step(d, x, fwd, back, cor, weight):
+    anywhere = pl.BlockSpec(memory_space=pl.ANY)
+    vmem = pl.BlockSpec(memory_space=pltpu.VMEM)
+    n, g = d.n, d.g
+    return pl.pallas_call(
+        functools.partial(grid_kernel, d),
+        name="grid",
+        out_shape=jax.ShapeDtypeStruct((d.el, n, g, d.pl, 2 * d.lb), BF16),
+        in_specs=[anywhere, anywhere, anywhere, vmem, vmem],
+        out_specs=anywhere,
+        scratch_shapes=[
+            pltpu.VMEM((2, g, d.half, 2 * d.lb), BF16),
+            pltpu.VMEM(fwd.shape, BF16),
+            pltpu.VMEM(back.shape, BF16),
+            pltpu.VMEM((g, 4 * d.kc, 2 * d.lb), F32),
+            pltpu.VMEM((g, 3 * d.kc, 2 * d.lb), BF16),
+            pltpu.VMEM((g, 3 * d.kc, 2 * d.lb), BF16),
+            pltpu.VMEM((g, 8, 2 * d.lb), F32),
+            pltpu.VMEM((d.el * g, d.half, 2 * d.lb), BF16),
+            pltpu.SemaphoreType.DMA((2,)),
+            pltpu.SemaphoreType.DMA((2,)),
+            pltpu.SemaphoreType.DMA((d.el * d.fields, n)),
+            pltpu.SemaphoreType.DMA((d.el * d.fields, n)),
+            pltpu.SemaphoreType.DMA((d.el * d.fields,)),
+        ],
+        compiler_params=pltpu.CompilerParams(
+            collective_id=2, has_side_effects=True, vmem_limit_bytes=VMEM_BYTES
+        ),
+    )(x, fwd, back, cor, weight)
+
+
+def analysis_kernel(
+    d, spectra, leg_hbm, state_hbm, spec_hbm, rate_hbm, quad, out, total_out,
+    leg, raw, damp, drift, recv, lhs, own, outer, cross, far, partial, bufs, rates, mix_rows, result, sums,
+    norms, band_norms, node_norms,
+    leg_sem, recv_sem, own_send, fwd_send, par_send, o_sem, x_sem, y_sem, buf_sem, res_sem, norm_sem,
+):
+    node = lax.axis_index("node")
+    band = lax.axis_index("band")
+    half, per, subs = d.degrees // 2, d.mc // 2, d.mc // SUB
+    total = d.nc * subs
+    is_outer = lax.rem(node, 3) == 0
+    beside = jnp.where(is_outer, 1 + node // 3, (node - 1) * 3)
+    other = jnp.where(is_outer, beside, 3 - node)
+    far_node = jnp.where(is_outer, 0, 3 - beside)
+
+    near = [("band", lax.rem(band + off, d.n)) for off in range(1, d.n)]
+    near += [("node", lax.rem(node + off, d.nnode)) for off in range(1, d.nnode)]
+    sem = pltpu.get_barrier_semaphore()
+    for axis, peer in near:
+        pl.semaphore_signal(sem, inc=1, device_id={axis: peer}, device_id_type=MESH)
+    pl.semaphore_wait(sem, len(near))
+
+    def copy(src, dst, send, recv_s, c, peer):
+        return pltpu.make_async_remote_copy(
+            src_ref=src.at[c], dst_ref=dst.at[c], send_sem=send.at[c], recv_sem=recv_s.at[c],
+            device_id={"node": peer}, device_id_type=MESH,
+        )
+
+    def to_inner(c):
+        return copy(own, outer, own_send, o_sem, c, beside)
+
+    def to_other(c):
+        return copy(own, cross, own_send, x_sem, c, other)
+
+    def forward(c):
+        return copy(outer, far, fwd_send, y_sem, c, other)
+
+    def to_outer(c):
+        return copy(partial, cross, par_send, x_sem, c, beside)
+
+    def fetch(i, slot):
+        return [
+            pltpu.make_async_copy(leg_hbm.at[pl.ds(i * SUB, SUB)], leg.at[slot], leg_sem.at[slot, 0]),
+            pltpu.make_async_copy(spec_hbm.at[0, :, pl.ds(i * SUB, SUB)], raw.at[slot, 0], leg_sem.at[slot, 1]),
+            pltpu.make_async_copy(state_hbm.at[:, pl.ds(i * SUB, SUB)], raw.at[slot, 1], leg_sem.at[slot, 2]),
+            pltpu.make_async_copy(rate_hbm.at[pl.ds(i * SUB, SUB)], damp.at[slot], leg_sem.at[slot, 3]),
+        ]
+
+    def fetch_spectra(c, slot):
+        return pltpu.make_async_copy(
+            spectra.at[:, :, :, pl.ds(c * per, per)], recv.at[slot], recv_sem.at[slot]
+        )
+
+    for copy_in in fetch(0, 0):
+        copy_in.start()
+    fetch_spectra(0, 0).start()
+
+    def chunk(c, _):
+        cslot = lax.rem(c, 2)
+
+        @pl.when(c + 1 < d.nc)
+        def _():
+            fetch_spectra(c + 1, 1 - cslot).start()
+
+        fetch_spectra(c, cslot).wait()
+        for s in range(d.el):
+            for lb in range(d.nlb):
+                for eg in range(d.eg):
+                    for f in range(d.fields):
+                        for p in range(2):
+                            for cc in range(2):
+                                r = (cc * d.members + eg * d.el + s) * d.fields + f
+                                tile = recv[cslot, s, lb * d.eg + eg, f * 4 + p * 2 + cc].astype(F32)
+                                for par in range(2):
+                                    at = ((par * d.nlb + lb) * d.rows + r) * d.mc + p * per
+                                    lhs[pl.ds(at, per), :] = tile[:, par * d.lb : (par + 1) * d.lb]
+
+        def sub(j, _):
+            i = c * subs + j
+            slot = lax.rem(i, 2)
+
+            @pl.when(i + 1 < total)
+            def _():
+                for copy_in in fetch(i + 1, 1 - slot):
+                    copy_in.start()
+
+            for copy_in in fetch(i, slot):
+                copy_in.wait()
+            for mi in range(SUB):
+                gather_rows(
+                    d,
+                    drift.at[mi],
+                    lambda cc, e: damp[slot, mi] * (raw[slot, 0, cc, mi, e] - raw[slot, 1, cc, mi, e]),
+                )
+            for mi in range(SUB):
+                for par in range(2):
+                    pieces = [
+                        lhs[
+                            pl.ds(
+                                (par * d.nlb + lb) * d.rows * d.mc + (mi % 2) * per + j * (SUB // 2) + mi // 2,
+                                d.rows,
+                                stride=d.mc,
+                            ),
+                            :,
+                        ]
+                        for lb in range(d.nlb)
+                    ]
+                    rows = jnp.concatenate(pieces, axis=1).astype(BF16)
+                    cols = slice(par * half, (par + 1) * half)
+                    y = mul(rows, leg[slot, mi, :, cols], ((1,), (0,)))
+                    own[c, j * SUB + mi, :, cols] = (y - drift[mi, :, cols]).astype(BF16)
+            return _
+
+        lax.fori_loop(0, subs, sub, None)
+
+        @pl.when(is_outer)
+        def _():
+            to_inner(c).start()
+
+        @pl.when(jnp.logical_not(is_outer))
+        def _():
+            to_other(c).start()
+
+            @pl.when(c >= 1)
+            def _():
+                to_inner(c - 1).wait_recv()
+                forward(c - 1).start()
+
+        return _
+
+    lax.fori_loop(0, d.nc, chunk, None)
+
+    @pl.when(jnp.logical_not(is_outer))
+    def _():
+        to_inner(d.nc - 1).wait_recv()
+        forward(d.nc - 1).start()
+
+    def load(c, slot):
+        at = pl.ds(c * d.mc, d.mc)
+        return [
+            pltpu.make_async_copy(state_hbm.at[:, at], bufs.at[slot, 0], buf_sem.at[slot, 0]),
+            pltpu.make_async_copy(spec_hbm.at[0, :, at], bufs.at[slot, 1], buf_sem.at[slot, 1]),
+            pltpu.make_async_copy(rate_hbm.at[at], rates.at[slot], buf_sem.at[slot, 2]),
+        ]
+
+    def save(c, slot):
+        return pltpu.make_async_copy(result.at[slot], out.at[0, :, pl.ds(c * d.mc, d.mc)], res_sem.at[slot])
+
+    for copy_in in load(0, 0):
+        copy_in.start()
+    sums[...] = jnp.zeros_like(sums)
+    q_own = quad[node, node]
+    q_total = quad[node, 0] + quad[node, 1] + quad[node, 2] + quad[node, 3]
+
+    def combine(c, _):
+        slot = lax.rem(c, 2)
+
+        @pl.when(c + 1 < d.nc)
+        def _():
+            for copy_in in load(c + 1, 1 - slot):
+                copy_in.start()
+
+        for copy_in in load(c, slot):
+            copy_in.wait()
+
+        @pl.when(c >= 2)
+        def _():
+            save(c - 2, slot).wait()
+
+        @pl.when(jnp.logical_not(is_outer))
+        def _():
+            to_other(c).wait_recv()
+            forward(c).wait_recv()
+
+            def mode(m, _):
+                a, b = own[c, m].astype(F32), cross[c, m].astype(F32)
+                o, y = outer[c, m].astype(F32), far[c, m].astype(F32)
+                mix = quad[beside, node] * a + quad[beside, other] * b + quad[beside, far_node] * y
+                partial[c, m] = mix.astype(BF16)
+                mix_rows[m] = (
+                    q_own * a + quad[node, other] * b + quad[node, beside] * o + quad[node, far_node] * y
+                )
+                return _
+
+            lax.fori_loop(0, d.mc, mode, None)
+            to_outer(c).start()
+
+        @pl.when(is_outer)
+        def _():
+            to_outer(c).wait_recv()
+
+            def mode(m, _):
+                mix_rows[m] = q_own * own[c, m].astype(F32) + cross[c, m].astype(F32)
+                return _
+
+            lax.fori_loop(0, d.mc, mode, None)
+
+        def update(m, _):
+            rate = rates[slot, m]
+            scale = q_own * rate
+            below = 1.0 + scale
+            changed, start = jnp.zeros_like(rate), jnp.zeros_like(rate)
+            for cc in range(2):
+                for e in range(d.members):
+                    r = (cc * d.members + e) * d.fields
+                    state, spec = bufs[slot, 0, cc, m, e], bufs[slot, 1, cc, m, e]
+                    mixed = mix_rows[m, r : r + d.fields, :] - q_total * (rate * state)
+                    new = (state + mixed + scale * spec) / below
+                    result[slot, cc, m, e] = new
+                    changed += (new - spec) * (new - spec)
+                    start += state * state
+            sums[0] += changed
+            sums[1] += start
+            return _
+
+        lax.fori_loop(0, d.mc, update, None)
+        save(c, slot).start()
+        return _
+
+    lax.fori_loop(0, d.nc, combine, None)
+    for c in range(max(d.nc - 2, 0), d.nc):
+        save(c, c % 2).wait()
+
+    def finish(c, _):
+        @pl.when(is_outer)
+        def _():
+            to_inner(c).wait_send()
+
+        @pl.when(jnp.logical_not(is_outer))
+        def _():
+            to_other(c).wait_send()
+            forward(c).wait_send()
+            to_outer(c).wait_send()
+
+        return _
+
+    lax.fori_loop(0, d.nc, finish, None)
+
+    def spread(axis, me, count, slots, k):
+        slots[me] = norms[k]
+        copies = [
+            pltpu.make_async_remote_copy(
+                src_ref=norms.at[k], dst_ref=slots.at[me],
+                send_sem=norm_sem.at[k, 0, off], recv_sem=norm_sem.at[k, 1, off],
+                device_id={axis: lax.rem(me + off, count)}, device_id_type=MESH,
+            )
+            for off in range(1, count)
+        ]
+        for each in copies:
+            each.start()
+        for each in copies:
+            each.wait()
+        return sum(slots[i] for i in range(count))
+
+    flat = sum(sums[:, :, k : k + LANES] for k in range(0, d.degrees, LANES))
+    norms[...] = jnp.zeros_like(norms)
+    for v in range(2):
+        norms[0, 4 * v : 4 * v + d.fields, :] = flat[v]
+    norms[1] = spread("band", band, d.n, band_norms, 0)
+    total_out[...] = spread("node", node, d.nnode, node_norms, 1)
+
+
+def analysis(d, spectra, legendre, state, iterate, rate, quadrature):
+    anywhere = pl.BlockSpec(memory_space=pl.ANY)
+    natural = (2, d.mc, d.members, d.fields, d.degrees)
+    block = pltpu.VMEM((d.nc, d.mc, d.rows, d.degrees), BF16)
+    dma = pltpu.SemaphoreType.DMA
+    return pl.pallas_call(
+        functools.partial(analysis_kernel, d),
+        name="analysis",
+        out_shape=(
+            jax.ShapeDtypeStruct(iterate.shape, F32),
+            jax.ShapeDtypeStruct((8, LANES), F32),
+        ),
+        in_specs=[anywhere] * 5 + [pl.BlockSpec(memory_space=pltpu.SMEM)],
+        out_specs=(anywhere, pl.BlockSpec(memory_space=pltpu.VMEM)),
+        scratch_shapes=[
+            pltpu.VMEM((2, SUB, d.hemi, d.degrees), BF16),
+            pltpu.VMEM((2, 2, 2, SUB, d.members, d.fields, d.degrees), F32),
+            pltpu.VMEM((2, SUB, d.fields, d.degrees), F32),
+            pltpu.VMEM((SUB, d.rows, d.degrees), F32),
+            pltpu.VMEM((2, d.el, d.n, d.g, d.mc // 2, 2 * d.lb), BF16),
+            pltpu.VMEM((2 * d.nlb * d.rows * d.mc, LANES), F32),
+            block,
+            block,
+            block,
+            block,
+            block,
+            pltpu.VMEM((2, 2) + natural, F32),
+            pltpu.VMEM((2, d.mc, d.fields, d.degrees), F32),
+            pltpu.VMEM((d.mc, d.rows, d.degrees), F32),
+            pltpu.VMEM((2,) + natural, F32),
+            pltpu.VMEM((2, d.fields, d.degrees), F32),
+            pltpu.VMEM((2, 8, LANES), F32),
+            pltpu.VMEM((d.n, 8, LANES), F32),
+            pltpu.VMEM((d.nnode, 8, LANES), F32),
+            dma((2, 4)),
+            dma((2,)),
+            dma((d.nc,)),
+            dma((d.nc,)),
+            dma((d.nc,)),
+            dma((d.nc,)),
+            dma((d.nc,)),
+            dma((d.nc,)),
+            dma((2, 3)),
+            dma((2,)),
+            dma((2, 2, d.n)),
+        ],
+        compiler_params=pltpu.CompilerParams(
+            collective_id=3, has_side_effects=True, vmem_limit_bytes=VMEM_BYTES
+        ),
+    )(spectra, legendre, state, iterate, rate, quadrature)
+
+
+def fast_body(d, state0, iterate, legendre, lat_weight, coriolis, damping, quadrature):
+    band = lax.axis_index("band")
+    first = (band // d.eg) * d.lb
+    cor = lax.dynamic_slice_in_dim(coriolis, first, d.lb, 1)
+    weight = jnp.tile(lax.dynamic_slice_in_dim(lat_weight, first, d.lb, 0), 2)[None]
+    x, forward, back = synthesis(d, iterate, legendre, jnp.asarray(trig_rows(d)))
+    x = x.reshape(d.el * d.g, d.half, 2 * d.lb)
+    spectra = grid_step(d, x, forward, back, cor, weight)
+    updated, norms = analysis(d, spectra, legendre, state0, iterate, damping, quadrature)
+    total = norms.reshape(2, 4, LANES)[:, : d.fields].sum(axis=2)
+    return updated, jnp.sqrt(total[0] / (total[1] + 1e-06))
+
+
 def solution(mesh):
     placed = (
         P(None, "band", None, None, None),
@@ -154,10 +901,16 @@
         P("band", None, None),
         P(),
     )
-    return jax.shard_map(
-        body,
-        mesh=mesh,
-        in_specs=placed,
-        out_specs=(P("node", None, "band", None, None, None), P()),
-        check_vma=False,
-    )
+
+    def call(*args):
+        d = Plan(mesh.shape["band"], mesh.shape["node"], args[1].shape, args[2].shape)
+        body = functools.partial(fast_body, d) if d.fits else plain_body
+        return jax.shard_map(
+            body,
+            mesh=mesh,
+            in_specs=placed,
+            out_specs=(P("node", None, "band", None, None, None), P()),
+            check_vma=False,
+        )(*args)
+
+    return call

time: 781 us -> 395 us (0.51); the launches traced: 770 us -> 393 us
  Pallas kernels: 0 us -> 360 us
  waiting for transfers between devices: 239 us -> 0 us
  local copies, waits for them, and re-layouts: 212 us -> 32.2 us
  matrix products: 173 us -> 0 us
  other arithmetic: 72.5 us -> 0.62 us
  blocking collectives: 38.3 us -> 0 us
  starting transfers between devices: 19.7 us -> 0 us
  between operations: 15.3 us -> 0.71 us
    pallas_call x0 -> x3, Pallas kernels: none -> 360 us  [the longest x1 184 us: analysis(): pl.pallas_call(functools.partial(analysis_kernel, d), name='analysis', ou...]
    all_gather x2 -> x0, waiting for transfers between devices: 217 us -> none  [analysis(): gathered = lax.all_gather(rest.astype(jnp.bfloat16), 'node')]
    dot_general x32 -> x0, matrix products: 173 us -> none  [the longest x28 67.6 us: mul(): lax.dot_general(a, b, (dims, ((), ())), preferred_element_type=jnp.float32)]
    reshape x16 -> x0, local copies, waits for them, and re-layouts: 153 us -> none  [the longest x4 49.5 us: analysis(): out = out.reshape(nband, 2, 2, pairs, 2, fields, ens, lat_rows)]
    psum x1 -> x0, blocking collectives: 38.3 us -> none  [body(): total = lax.psum(jnp.stack([change, base]), ('node', 'band'))]
    slice x5 -> x0, local copies, waits for them, and re-layouts: 22.2 us -> none  [the longest x2 14.5 us: analysis(): both[:, 0]]
    add x17 -> x0, other arithmetic: 21.6 us -> none  [the longest x2 13.3 us: analysis(): sum((quad_row[p] * gathered[p].astype(jnp.float32) for p in range(nnode)))]
    all_to_all x4 -> x0, waiting for transfers between devices: 20.7 us -> none  [the longest x2 15.6 us: synthesis(): return lax.all_to_all(four, 'band', split_axis=0, concat_axis=0, tiled=True)]
  transfers between devices with their start and end apart: 6 -> 0, of which waited for: 4 -> 0; matrix products, arithmetic and copies ran while one was open for 28% -> 0% of each run, Pallas kernels for 0% -> 0%
where the time goes in v1:
time: 395 us; the launch traced here: 393 us
  Pallas kernels  360 us (91%)
  local copies, waits for them, and re-layouts  32.2 us (8%)
    pallas_call x1, Pallas kernels, analysis(): pl.pallas_call(functools.partial(analysis_kernel, d), name='analysis', ou...  184 us
    pallas_call x1, Pallas kernels, grid_step(): pl.pallas_call(functools.partial(grid_kernel, d), name='grid', out_shape=...  90.1 us
    pallas_call x1, Pallas kernels, synthesis(): pl.pallas_call(functools.partial(synthesis_kernel, d), name='synthesis',...  85.3 us
    unnamed x12, local copies, waits for them, and re-layouts  30.3 us

profile of v1, /device:TPU:0, one launch (start us, length us, event | category | flops | bytes accessed | tf_op | source)
XLA Modules:
  0.0 393.4 jit_solution(17510967307259967992)
XLA Ops:
  0.6 0.0 copy-start
  0.7 0.8 dynamic_slice.7
  1.4 0.6 tile.2
  2.0 0.0 copy-done
  2.0 0.6 constant_dynamic-slice_fusion.cor
  2.6 9.7 %copy.10.it_hbm.spec_hbm = f32[1,2,128,4,3,512]{5,4,3,2,1,0:T(4,128)} copy(f32[1,2,128,4,3,512]{5,3,4,2,1,0:T(4,128)} %param.9) | data formatting | bytes 12582912 | tf_op args[1]
  12.3 85.3 %synthesis.1 = (bf16[24,8,64,256]{3,2,1,0:T(8,128)(2,1)}, bf16[2,2,3,704,512]{4,3,2,1,0:T(8,128)(2,1)}, bf16[2,2,1024,512]{3,2,1,0:T(8,128)(2,1)}) custom-call(f32[1,2,128,4,3,512]{5,4,3,2,1,0:T(4,128)} %copy.10.it_hbm.spec_hbm, bf16[128,512,512]{2,1,0:T(8,128)(2,1)} %leg_hbm.3, f32[2,162,512]{2,1,0:T(8,128)} %constant.29.clone.trig), custom_call_target="tpu_custom_call" | custom-call | tf_op jit(solution)/shard_map/synthesis/pallas_call | solution.py:362
  97.6 90.1 %grid.1.spectra = bf16[2,8,12,64,256]{4,3,2,1,0:T(8,128)(2,1)} custom-call(bf16[24,512,256]{2,1,0:T(8,128)(2,1)} %bitcast.5, bf16[2,2,3,704,512]{4,3,2,1,0:T(8,128)(2,1)} %get-tuple-element.8.fwd_hbm, bf16[2,2,1024,512]{3,2,1,0:T(8,128)(2,1)} %get-tuple-element.9.back_hbm, f32[2,128]{1,0:T(2,128)} %constant_dynamic-slice_fusion.cor, f32[1,256]{1,0:T(1,128)} %bitcast.7), custom_call_target="tpu_custom_call" | custom-call | tf_op jit(solution)/shard_map/grid/pallas_call | solution.py:540
  187.7 0.0 copy-start.2
  187.7 9.8 %copy.11.state_hbm = f32[2,128,4,3,512]{4,3,2,1,0:T(4,128)} copy(f32[2,128,4,3,512]{4,2,3,1,0:T(4,128)} %param.8) | data formatting | bytes 12582912 | tf_op args[0]
  197.5 0.0 copy-done.2
  197.5 1.5 copy.13.rate_hbm
  199.0 184.5 %analysis.1 = (f32[1,2,128,4,3,512]{5,4,3,2,1,0:T(4,128)}, f32[8,128]{1,0:T(8,128)}) custom-call(bf16[2,8,12,64,256]{4,3,2,1,0:T(8,128)(2,1)} %grid.1.spectra, bf16[128,512,512]{2,1,0:T(8,128)(2,1)} %leg_hbm.3, f32[2,128,4,3,512]{4,3,2,1,0:T(4,128)} %copy.11.state_hbm, f32[1,2,128,4,3,512]{5,4,3,2,1,0:T(4,128)} %copy.10.it_hbm.spec_hbm, ...), custom_call_target="tpu_custom_call" | custom-call | tf_op jit(solution)/shard_map/analysis/pallas_call | solution.py:834
  383.5 0.0 copy-start.1
  383.5 0.0 copy-start.3
  383.5 9.2 %copy.14 = f32[1,2,128,4,3,512]{5,3,4,2,1,0:T(4,128)} copy(f32[1,2,128,4,3,512]{5,4,3,2,1,0:T(4,128)} %get-tuple-element.12) | data formatting | bytes 12582912
  392.8 0.0 copy-done.3
  392.8 0.1 slice_reduce_fusion
  392.9 0.5 sqrt_bitcast_fusion
  393.4 0.0 copy-done.1
Async XLA Ops:
  0.6 1.4 copy-start
  187.7 9.8 %copy-start.2 = (f32[128,3,512]{2,0,1:T(8,128)S(1)}, f32[128,3,512]{2,0,1:T(8,128)}, u32[]{:S(2)}) copy-start(f32[128,3,512]{2,0,1:T(8,128)} %param.13) | copy-start | bytes 2359300
  383.5 9.9 %copy-start.1 = (f32[2,512]{1,0:T(2,128)S(1)}, f32[2,512]{1,0:T(2,128)}, u32[]{:S(2)}) copy-start(f32[2,512]{1,0:T(2,128)} %param.12) | copy-start | bytes 12292
  383.5 9.2 %copy-start.3 = (f32[8,128]{1,0:T(8,128)S(1)}, f32[8,128]{1,0:T(8,128)}, u32[]{:S(2)}) copy-start(f32[8,128]{1,0:T(8,128)} %get-tuple-element.11) | copy-start | bytes 12292

commit v2 on v0

--- a/solution.py
+++ b/solution.py
@@ -1,9 +1,19 @@
+import functools
 import math
 
 import jax
 import jax.numpy as jnp
+import numpy as np
 from jax import lax
+from jax.experimental import pallas as pl
+from jax.experimental.pallas import tpu as pltpu
 from jax.sharding import PartitionSpec as P
+
+MESH = pl.DeviceIdType.MESH
+F32, BF16 = jnp.float32, jnp.bfloat16
+VMEM_BYTES = 63_000_000
+LANES = 128
+SUB = 4
 
 
 def split_bf16(x):
@@ -40,7 +50,7 @@
     return lax.dot_general(a, b, (dims, ((), ())), preferred_element_type=jnp.float32)
 
 
-def body(state0, iterate, legendre, lat_weight, coriolis, damping, quadrature):
+def plain_body(state0, iterate, legendre, lat_weight, coriolis, damping, quadrature):
     spec = iterate[0]
     degrees = legendre.shape[2]
     half = degrees // 2
@@ -144,6 +154,730 @@
     return (updated[None], ratio)
 
 
+class Plan:
+    def __init__(self, nband, nnode, iterate, legendre):
+        self.n, self.nnode = nband, nnode
+        self.modes, self.members, self.fields, self.degrees = iterate[2:]
+        self.hemi = legendre[1]
+        self.ml = self.modes // nband
+        self.lb = LANES
+        self.nlb = self.hemi // self.lb
+        self.eg = max(nband // max(self.nlb, 1), 1)
+        self.el = self.members // self.eg
+        self.rows = 2 * self.members * self.fields
+        self.pl = self.ml // 2
+        self.mc = 16
+        self.nc = self.ml // self.mc
+        self.half = self.modes // 2
+        self.kc = (self.half + 16) // 3
+        self.g = 4 * self.fields
+        self.fits = (
+            nnode == 4
+            and self.fields == 3
+            and self.nlb * self.eg == nband
+            and self.eg * self.el == self.members
+            and self.hemi % self.lb == 0
+            and self.ml % self.mc == 0
+            and self.modes % nband == 0
+            and (self.half + 16) % 48 == 0
+            and self.rows % 8 == 0
+            and self.degrees % 256 == 0
+        )
+
+
+def gather_rows(d, rows, piece):
+    for cc in range(2):
+        for f in range(d.fields):
+            r = (cc * d.fields + f) * d.members
+            rows[r : r + d.members, :] = piece(cc, f)
+
+
+def build_tables(d, trig, fwd, back):
+    tall, fine = 3 * d.kc // 16, 16
+    short = d.half // 16
+
+    def turn(big, small):
+        cb, sb, cs, ss = trig[0, big], trig[1, big], trig[0, small], trig[1, small]
+        return cb * cs - sb * ss, -(sb * cs + cb * ss)
+
+    for p in range(2):
+        ramp = (2 * lax.broadcasted_iota(jnp.int32, (1, d.half), 1) + p).astype(F32) * (1.0 / d.modes)
+
+        def ahead(a, _):
+            cos, sin = turn(pl.ds(p * tall + a, 1), pl.ds((2 * tall + short + p * fine), fine))
+            inside = lax.broadcasted_iota(jnp.int32, (fine, 1), 0) + a * fine <= d.half
+            cos, sin = jnp.where(inside, cos, 0.0), jnp.where(inside, sin, 0.0)
+            c = a // (d.kc // 16)
+            at = (a - c * (d.kc // 16)) * 16
+            for cc, pair in enumerate(((cos, ramp * sin), (sin, -ramp * cos))):
+                for v, t in enumerate(pair):
+                    top = t.astype(BF16)
+                    fwd[p, cc, c, pl.ds(pl.multiple_of(2 * v * d.kc + at, 16), 16)] = top
+                    fwd[p, cc, c, pl.ds(pl.multiple_of((2 * v + 1) * d.kc + at, 16), 16)] = (
+                        t - top.astype(F32)
+                    ).astype(BF16)
+            return _
+
+        lax.fori_loop(0, tall, ahead, None)
+        first = jnp.where(lax.broadcasted_iota(jnp.int32, (1, d.half), 1) == 0, 0.5, 1.0)
+
+        def behind(a, _):
+            pair = turn(pl.ds(2 * tall + a, 1), pl.ds(2 * tall + short + (2 + p) * fine, fine))
+            for cc, t in enumerate(pair):
+                t = t * first
+                top = t.astype(BF16)
+                at = pl.multiple_of(a * 16, 16)
+                back[p, cc, pl.ds(at, 16)] = top
+                back[p, cc, pl.ds(pl.multiple_of(d.half + at, 16), 16)] = (t - top.astype(F32)).astype(BF16)
+            return _
+
+        lax.fori_loop(0, short, behind, None)
+
+
+def trig_rows(d):
+    points = 2 * d.modes
+    tall, short = 3 * d.kc // 16, d.half // 16
+    wave = 2 * np.arange(d.half)
+    k = np.arange(d.half)
+    big = [16 * np.arange(tall)[:, None] * (wave + p)[None] for p in range(2)]
+    big.append(32 * np.arange(short)[:, None] * k[None])
+    small = [np.arange(16)[:, None] * (wave + p)[None] for p in range(2)]
+    small += [(2 * np.arange(16) + p)[:, None] * k[None] for p in range(2)]
+    angle = np.concatenate(big + small) % points * (2.0 * np.pi / points)
+    scale = np.where(np.arange(len(angle)) < 2 * tall + short, d.modes**-0.5, 1.0)[:, None]
+    return np.stack([np.cos(angle) * scale, np.sin(angle) * scale]).astype(np.float32)
+
+
+def four_points(ce, se, co, so):
+    a, b, c, e = ce + se, ce - se, co + so, co - so
+    return a + c, b + e, a - c, b - e
+
+
+def fold_points(t):
+    s13, s24, d13, d24 = t[0] + t[2], t[1] + t[3], t[0] - t[2], t[1] - t[3]
+    return s13 + s24, s13 - s24, d13 + d24, d13 - d24
+
+
+def sweep_kernel(
+    d, it_hbm, leg_hbm, state_hbm, rate_hbm, trig, cor, weight, quad,
+    out, total_out, x_hbm, spectra,
+    send, fwd, back, send_back, outer, cross, far, sums, norms, band_norms, node_norms,
+    leg_sem, a_send, a_recv, a_own, x_sem, b_send, b_recv, b_own, recv_sem,
+    own_send, fwd_send, par_send, o_sem, x_recv, y_sem, buf_sem, res_sem, norm_sem,
+):
+    band, node = lax.axis_index("band"), lax.axis_index("node")
+    n, g, half = d.n, d.g, d.degrees // 2
+    per, subs = d.mc // 2, d.mc // SUB
+    total = d.nc * subs
+    last = d.el - 1
+
+    near = [("band", lax.rem(band + off, n)) for off in range(1, n)]
+    near += [("node", lax.rem(node + off, d.nnode)) for off in range(1, d.nnode)]
+    sem = pltpu.get_barrier_semaphore()
+    for axis, peer in near:
+        pl.semaphore_signal(sem, inc=1, device_id={axis: peer}, device_id_type=MESH)
+    pl.semaphore_wait(sem, len(near))
+
+    def ahead(s, c, off):
+        peer = lax.rem(band + off, n)
+        return pltpu.make_async_remote_copy(
+            src_ref=send.at[c, s, peer],
+            dst_ref=x_hbm.at[pl.ds(s * g, g), band, pl.ds(c * per, per)],
+            send_sem=a_send.at[s * d.nc + c, off],
+            recv_sem=a_recv.at[s * d.nc + c, off],
+            device_id={"band": peer},
+            device_id_type=MESH,
+        )
+
+    def ahead_own(s, c):
+        return pltpu.make_async_copy(
+            send.at[c, s, band], x_hbm.at[pl.ds(s * g, g), band, pl.ds(c * per, per)], a_own.at[s * d.nc + c]
+        )
+
+    def start_ahead(s, c):
+        for off in range(1, n):
+            ahead(s, c, off).start()
+        ahead_own(s, c).start()
+
+    def synthesis(raw, rows, leg, stage):
+        def fetch(i, slot):
+            return [
+                pltpu.make_async_copy(leg_hbm.at[pl.ds(i * SUB, SUB)], leg.at[slot], leg_sem.at[slot, 0]),
+                pltpu.make_async_copy(it_hbm.at[0, :, pl.ds(i * SUB, SUB)], raw.at[slot], leg_sem.at[slot, 1]),
+            ]
+
+        for copy_in in fetch(0, 0):
+            copy_in.start()
+
+        def chunk(c, _):
+            def sub(j, _):
+                i = c * subs + j
+                slot = lax.rem(i, 2)
+
+                @pl.when(i + 1 < total)
+                def _():
+                    for copy_in in fetch(i + 1, 1 - slot):
+                        copy_in.start()
+
+                for copy_in in fetch(i, slot):
+                    copy_in.wait()
+                for mi in range(SUB):
+                    gather_rows(d, rows.at[mi], lambda cc, f: raw[slot, cc, mi, f])
+                for mi in range(SUB):
+                    x = rows[mi].astype(BF16)
+                    table = leg[slot, mi]
+                    for par in range(2):
+                        cols = slice(par * half, (par + 1) * half)
+                        y = mul(x[:, cols], table[:, cols], ((1,), (1,)))
+                        for lb in range(d.nlb):
+                            at = (lb * 2 + par) * d.rows * d.mc + (mi % 2) * per + j * (SUB // 2) + mi // 2
+                            stage[pl.ds(at, d.rows, stride=d.mc), :] = y[:, lb * LANES : (lb + 1) * LANES]
+                return _
+
+            lax.fori_loop(0, subs, sub, None)
+            for s in range(d.el):
+                for f in range(d.fields):
+                    for p in range(2):
+                        for cc in range(2):
+                            for lb in range(d.nlb):
+                                for eg in range(d.eg):
+                                    r = (cc * d.fields + f) * d.members + eg * d.el + s
+                                    tiles = [
+                                        stage[pl.ds(((lb * 2 + par) * d.rows + r) * d.mc + p * per, per), :]
+                                        for par in range(2)
+                                    ]
+                                    send[c, s, lb * d.eg + eg, (f * 2 + p) * 2 + cc] = jnp.concatenate(
+                                        tiles, axis=1
+                                    ).astype(BF16)
+            start_ahead(0, c)
+            return _
+
+        lax.fori_loop(0, d.nc, chunk, None)
+
+    pl.run_scoped(
+        synthesis,
+        pltpu.VMEM((2, 2, SUB, d.fields, d.members, d.degrees), F32),
+        pltpu.VMEM((SUB, d.rows, d.degrees), F32),
+        pltpu.VMEM((2, SUB, d.hemi, d.degrees), BF16),
+        pltpu.VMEM((2 * d.nlb * d.rows * d.mc, LANES), F32),
+    )
+    if d.el > 1:
+
+        def rest(i, _):
+            start_ahead(1 + i // d.nc, lax.rem(i, d.nc))
+            return _
+
+        lax.fori_loop(0, last * d.nc, rest, None)
+    build_tables(d, trig, fwd, back)
+
+    def behind(s, f, off):
+        peer = lax.rem(band + off, n)
+        k = s * d.fields + f
+        return pltpu.make_async_remote_copy(
+            src_ref=send_back.at[pl.ds(s * g + f * 4, 4), pl.ds(peer * d.pl, d.pl)],
+            dst_ref=spectra.at[s, band, pl.ds(f * 4, 4)],
+            send_sem=b_send.at[k, off],
+            recv_sem=b_recv.at[k, off],
+            device_id={"band": peer},
+            device_id_type=MESH,
+        )
+
+    def behind_own(s, f):
+        return pltpu.make_async_copy(
+            send_back.at[pl.ds(s * g + f * 4, 4), pl.ds(band * d.pl, d.pl)],
+            spectra.at[s, band, pl.ds(f * 4, 4)],
+            b_own.at[s * d.fields + f],
+        )
+
+    def final(c, off):
+        peer = lax.rem(band + off, n)
+        k = last * d.fields + c
+        return pltpu.make_async_remote_copy(
+            src_ref=send_back.at[pl.ds(last * g, g), pl.ds(peer * d.pl + c * per, per)],
+            dst_ref=spectra.at[last, band, :, pl.ds(c * per, per)],
+            send_sem=b_send.at[k, off],
+            recv_sem=b_recv.at[k, off],
+            device_id={"band": peer},
+            device_id_type=MESH,
+        )
+
+    def final_own(c):
+        return pltpu.make_async_copy(
+            send_back.at[pl.ds(last * g, g), pl.ds(band * d.pl + c * per, per)],
+            spectra.at[last, band, :, pl.ds(c * per, per)],
+            b_own.at[last * d.fields + c],
+        )
+
+    def grid(x, part, high, low, edge):
+        kc, lb = d.kc, d.lb
+
+        def step(s, _):
+            def arrive(c, _):
+                for off in range(1, n):
+                    ahead(s, c, off).wait_recv()
+                ahead_own(s, c).wait()
+                return _
+
+            lax.fori_loop(0, d.nc, arrive, None)
+            fetch = pltpu.make_async_copy(x_hbm.at[pl.ds(s * g, g)], x, x_sem.at[0])
+            fetch.start()
+            fetch.wait()
+
+            def rows(c, _):
+                def field(f, _):
+                    for p in range(2):
+                        for cc in range(2):
+                            q = p * 2 + cc
+                            y = mul(fwd[p, cc, c], x[f * 4 + q].reshape(d.half, 2 * lb), ((1,), (0,)))
+                            part[f * 4 + q, :kc] = y[:kc] + y[kc : 2 * kc]
+                            part[f * 4 + q, kc:] = y[2 * kc : 3 * kc] + y[3 * kc :]
+                    return _
+
+                lax.fori_loop(0, d.fields, field, None)
+
+                def block(i, _):
+                    def load(f, q, v):
+                        return part[f * 4 + q, pl.ds(pl.multiple_of(v * kc + i * 16, 16), 16)]
+
+                    folded = []
+                    comps = [[[load(f, q, v) for q in range(4)] for v in range(2)] for f in range(d.fields)]
+                    for h in range(2):
+                        val, slo = [], []
+                        for f in range(d.fields):
+                            hemi = [
+                                [a[:, :lb] + a[:, lb:] if h == 0 else a[:, :lb] - a[:, lb:] for a in comps[f][v]]
+                                for v in range(2)
+                            ]
+                            val.append(four_points(*hemi[0]))
+                            g0, g1, g2, g3 = hemi[1]
+                            slo.append(four_points(g1, g0, g3, g2))
+                        c_lat = cor[h : h + 1]
+                        tend = [[], [], []]
+                        for k in range(4):
+                            u, w, z = (val[f][k] for f in range(3))
+                            du, dw, dz = (slo[f][k] for f in range(3))
+                            tend[0].append(c_lat * w - u * du - dz)
+                            tend[1].append(-u * dw - c_lat * u)
+                            tend[2].append(-u * dz - (1.0 + z) * du)
+                        folded.append([fold_points(t) for t in tend])
+                    at = pl.multiple_of(c * kc + i * 16, 16)
+                    for f in range(d.fields):
+                        for q in range(4):
+                            north, south = folded[0][f][q], folded[1][f][q]
+                            t = jnp.concatenate([north + south, north - south], axis=1)
+                            top = t.astype(BF16)
+                            high[f * 4 + q, pl.ds(at, 16)] = top
+                            low[f * 4 + q, pl.ds(at, 16)] = (t - top.astype(F32)).astype(BF16)
+                            edge[f * 4 + q] = t[:8]
+                    return _
+
+                lax.fori_loop(0, kc // 16, block, None)
+                return _
+
+            lax.fori_loop(0, 3, rows, None)
+
+            def field(f, _):
+                for q in range(4):
+                    p, cc = divmod(q, 2)
+                    both = mul(back[p, cc], high[f * 4 + q, : d.half], ((1,), (0,)))
+                    spec = both[: d.half] + both[d.half :]
+                    spec = spec + mul(back[p, cc, : d.half], low[f * 4 + q, : d.half], ((1,), (0,)))
+                    if p == cc:
+                        sign = 1.0 - 2.0 * (lax.broadcasted_iota(jnp.int32, (d.half, 1), 0) % 2).astype(F32)
+                        scale = 0.5 / math.sqrt(d.modes) * (1.0 if p == 0 else -1.0)
+                        spec = spec + (sign * scale) * edge[f * 4 + q, :1]
+                    send_back[s * g + f * 4 + q] = (spec * weight[...]).astype(BF16)
+
+                @pl.when(s < last)
+                def _():
+                    for off in range(1, n):
+                        behind(s, f, off).start()
+                    behind_own(s, f).start()
+
+                return _
+
+            lax.fori_loop(0, d.fields, field, None)
+            return _
+
+        lax.fori_loop(0, d.el, step, None)
+
+        def chunk(c, _):
+            for off in range(1, n):
+                final(c, off).start()
+            final_own(c).start()
+            return _
+
+        lax.fori_loop(0, d.nc, chunk, None)
+
+    pl.run_scoped(
+        grid,
+        pltpu.VMEM((g, n, d.pl, 2 * d.lb), BF16),
+        pltpu.VMEM((g, 2 * d.kc, 2 * d.lb), F32),
+        pltpu.VMEM((g, 3 * d.kc, 2 * d.lb), BF16),
+        pltpu.VMEM((g, 3 * d.kc, 2 * d.lb), BF16),
+        pltpu.VMEM((g, 8, 2 * d.lb), F32),
+    )
+
+    is_outer = lax.rem(node, 3) == 0
+    is_inner = jnp.logical_not(is_outer)
+    beside = jnp.where(is_outer, 1 + node // 3, (node - 1) * 3)
+    other = jnp.where(is_outer, beside, 3 - node)
+    far_node = jnp.where(is_outer, 0, 3 - beside)
+
+    def analysis(leg, raw, damp, drift, recv, lhs, own, partial, bufs, rates, mix_rows, result):
+        def copy(src, dst, send_s, recv_s, c, peer):
+            return pltpu.make_async_remote_copy(
+                src_ref=src.at[c], dst_ref=dst.at[c], send_sem=send_s.at[c], recv_sem=recv_s.at[c],
+                device_id={"node": peer}, device_id_type=MESH,
+            )
+
+        def to_inner(c):
+            return copy(own, outer, own_send, o_sem, c, beside)
+
+        def to_other(c):
+            return copy(own, cross, own_send, x_recv, c, other)
+
+        def forward(c):
+            return copy(outer, far, fwd_send, y_sem, c, other)
+
+        def to_outer(c):
+            return copy(partial, cross, par_send, x_recv, c, beside)
+
+        def fetch(i, slot):
+            at = pl.ds(i * SUB, SUB)
+            return [
+                pltpu.make_async_copy(leg_hbm.at[at], leg.at[slot], leg_sem.at[slot, 0]),
+                pltpu.make_async_copy(it_hbm.at[0, :, at], raw.at[slot, 0], leg_sem.at[slot, 1]),
+                pltpu.make_async_copy(state_hbm.at[:, at], raw.at[slot, 1], leg_sem.at[slot, 2]),
+                pltpu.make_async_copy(rate_hbm.at[:, at], damp.at[slot], leg_sem.at[slot, 3]),
+            ]
+
+        def fetch_spectra(c, slot):
+            return pltpu.make_async_copy(
+                spectra.at[:, :, :, pl.ds(c * per, per)], recv.at[slot], recv_sem.at[slot]
+            )
+
+        def arrive(c):
+            for off in range(1, n):
+                final(c, off).wait_recv()
+            final_own(c).wait()
+
+        for copy_in in fetch(0, 0):
+            copy_in.start()
+
+        def early(i, _):
+            s, f = i // d.fields, lax.rem(i, d.fields)
+            for off in range(1, n):
+                behind(s, f, off).wait_recv()
+            behind_own(s, f).wait()
+            return _
+
+        lax.fori_loop(0, last * d.fields, early, None)
+        arrive(0)
+        fetch_spectra(0, 0).start()
+
+        def chunk(c, _):
+            cslot = lax.rem(c, 2)
+            fetch_spectra(c, cslot).wait()
+            for s in range(d.el):
+                for lb in range(d.nlb):
+                    for eg in range(d.eg):
+                        for f in range(d.fields):
+                            for p in range(2):
+                                for cc in range(2):
+                                    r = (cc * d.fields + f) * d.members + eg * d.el + s
+                                    tile = recv[cslot, s, lb * d.eg + eg, f * 4 + p * 2 + cc].astype(F32)
+                                    for par in range(2):
+                                        at = ((par * d.nlb + lb) * d.rows + r) * d.mc + p * per
+                                        lhs[pl.ds(at, per), :] = tile[:, par * d.lb : (par + 1) * d.lb]
+
+            def sub(j, _):
+                i = c * subs + j
+                slot = lax.rem(i, 2)
+
+                @pl.when(i + 1 < total)
+                def _():
+                    for copy_in in fetch(i + 1, 1 - slot):
+                        copy_in.start()
+
+                for copy_in in fetch(i, slot):
+                    copy_in.wait()
+                for mi in range(SUB):
+                    gather_rows(
+                        d,
+                        drift.at[mi],
+                        lambda cc, f: damp[slot, f, mi : mi + 1] * (raw[slot, 0, cc, mi, f] - raw[slot, 1, cc, mi, f]),
+                    )
+                for mi in range(SUB):
+                    for par in range(2):
+                        pieces = [
+                            lhs[
+                                pl.ds(
+                                    (par * d.nlb + lb) * d.rows * d.mc + (mi % 2) * per + j * (SUB // 2) + mi // 2,
+                                    d.rows,
+                                    stride=d.mc,
+                                ),
+                                :,
+                            ]
+                            for lb in range(d.nlb)
+                        ]
+                        rows = jnp.concatenate(pieces, axis=1).astype(BF16)
+                        cols = slice(par * half, (par + 1) * half)
+                        y = mul(rows, leg[slot, mi, :, cols], ((1,), (0,)))
+                        own[c, j * SUB + mi, :, cols] = (y - drift[mi, :, cols]).astype(BF16)
+                return _
+
+            lax.fori_loop(0, subs, sub, None)
+
+            @pl.when(is_outer)
+            def _():
+                to_inner(c).start()
+
+            @pl.when(is_inner)
+            def _():
+                to_other(c).start()
+
+                @pl.when(c >= 1)
+                def _():
+                    to_inner(c - 1).wait_recv()
+                    forward(c - 1).start()
+
+            @pl.when(c + 1 < d.nc)
+            def _():
+                arrive(c + 1)
+                fetch_spectra(c + 1, 1 - cslot).start()
+
+            return _
+
+        lax.fori_loop(0, d.nc, chunk, None)
+
+        @pl.when(is_inner)
+        def _():
+            to_inner(d.nc - 1).wait_recv()
+            forward(d.nc - 1).start()
+
+        def load(c, slot):
+            at = pl.ds(c * d.mc, d.mc)
+            return [
+                pltpu.make_async_copy(state_hbm.at[:, at], bufs.at[slot, 0], buf_sem.at[slot, 0]),
+                pltpu.make_async_copy(it_hbm.at[0, :, at], bufs.at[slot, 1], buf_sem.at[slot, 1]),
+                pltpu.make_async_copy(rate_hbm.at[:, at], rates.at[slot], buf_sem.at[slot, 2]),
+            ]
+
+        def save(c, slot):
+            return pltpu.make_async_copy(result.at[slot], out.at[0, :, pl.ds(c * d.mc, d.mc)], res_sem.at[slot])
+
+        for copy_in in load(0, 0):
+            copy_in.start()
+        sums[...] = jnp.zeros_like(sums)
+        q_own = quad[node, node]
+        q_total = quad[node, 0] + quad[node, 1] + quad[node, 2] + quad[node, 3]
+
+        def combine(c, _):
+            slot = lax.rem(c, 2)
+
+            @pl.when(c + 1 < d.nc)
+            def _():
+                for copy_in in load(c + 1, 1 - slot):
+                    copy_in.start()
+
+            for copy_in in load(c, slot):
+                copy_in.wait()
+
+            @pl.when(c >= 2)
+            def _():
+                save(c - 2, slot).wait()
+
+            @pl.when(is_inner)
+            def _():
+                to_other(c).wait_recv()
+                forward(c).wait_recv()
+
+                def mode(m, _):
+                    a, b = own[c, m].astype(F32), cross[c, m].astype(F32)
+                    o, y = outer[c, m].astype(F32), far[c, m].astype(F32)
+                    mix = quad[beside, node] * a + quad[beside, other] * b + quad[beside, far_node] * y
+                    partial[c, m] = mix.astype(BF16)
+                    mix_rows[m] = (
+                        q_own * a + quad[node, other] * b + quad[node, beside] * o + quad[node, far_node] * y
+                    )
+                    return _
+
+                lax.fori_loop(0, d.mc, mode, None)
+                to_outer(c).start()
+
+            @pl.when(is_outer)
+            def _():
+                to_outer(c).wait_recv()
+
+                def mode(m, _):
+                    mix_rows[m] = q_own * own[c, m].astype(F32) + cross[c, m].astype(F32)
+                    return _
+
+                lax.fori_loop(0, d.mc, mode, None)
+
+            def update(m, _):
+                for f in range(d.fields):
+                    rate = rates[slot, f, pl.ds(m, 1)]
+                    scale = q_own * rate
+                    below = 1.0 + scale
+                    pull = q_total * rate
+                    changed, start = sums[0, f], sums[1, f]
+                    for cc in range(2):
+                        r = (cc * d.fields + f) * d.members
+                        state, spec = bufs[slot, 0, cc, m, f], bufs[slot, 1, cc, m, f]
+                        mixed = mix_rows[m, r : r + d.members, :] - pull * state
+                        new = (state + mixed + scale * spec) / below
+                        result[slot, cc, m, f] = new
+                        changed += (new - spec) * (new - spec)
+                        start += state * state
+                    sums[0, f] = changed
+                    sums[1, f] = start
+                return _
+
+            lax.fori_loop(0, d.mc, update, None)
+            save(c, slot).start()
+            return _
+
+        lax.fori_loop(0, d.nc, combine, None)
+        for c in range(max(d.nc - 2, 0), d.nc):
+            save(c, c % 2).wait()
+
+        def finish(c, _):
+            @pl.when(is_outer)
+            def _():
+                to_inner(c).wait_send()
+
+            @pl.when(is_inner)
+            def _():
+                to_other(c).wait_send()
+                forward(c).wait_send()
+                to_outer(c).wait_send()
+
+            for off in range(1, n):
+                final(c, off).wait_send()
+                for s in range(d.el):
+                    ahead(s, c, off).wait_send()
+            return _
+
+        lax.fori_loop(0, d.nc, finish, None)
+
+        def finish_early(i, _):
+            for off in range(1, n):
+                behind(i // d.fields, lax.rem(i, d.fields), off).wait_send()
+            return _
+
+        lax.fori_loop(0, last * d.fields, finish_early, None)
+
+    natural = (2, d.mc, d.fields, d.members, d.degrees)
+    pl.run_scoped(
+        analysis,
+        pltpu.VMEM((2, SUB, d.hemi, d.degrees), BF16),
+        pltpu.VMEM((2, 2, 2, SUB, d.fields, d.members, d.degrees), F32),
+        pltpu.VMEM((2, d.fields, SUB, d.degrees), F32),
+        pltpu.VMEM((SUB, d.rows, d.degrees), F32),
+        pltpu.VMEM((2, d.el, n, g, per, 2 * d.lb), BF16),
+        pltpu.VMEM((2 * d.nlb * d.rows * d.mc, LANES), F32),
+        pltpu.VMEM((d.nc, d.mc, d.rows, d.degrees), BF16),
+        pltpu.VMEM((d.nc, d.mc, d.rows, d.degrees), BF16),
+        pltpu.VMEM((2, 2) + natural, F32),
+        pltpu.VMEM((2, d.fields, d.mc, d.degrees), F32),
+        pltpu.VMEM((d.mc, d.rows, d.degrees), F32),
+        pltpu.VMEM((2,) + natural, F32),
+    )
+
+    def spread(axis, me, count, slots, k):
+        slots[me] = norms[k]
+        copies = [
+            pltpu.make_async_remote_copy(
+                src_ref=norms.at[k], dst_ref=slots.at[me],
+                send_sem=norm_sem.at[k, 0, off], recv_sem=norm_sem.at[k, 1, off],
+                device_id={axis: lax.rem(me + off, count)}, device_id_type=MESH,
+            )
+            for off in range(1, count)
+        ]
+        for each in copies:
+            each.start()
+        for each in copies:
+            each.wait()
+        return sum(slots[i] for i in range(count))
+
+    norms[...] = jnp.zeros_like(norms)
+    for v in range(2):
+        for f in range(d.fields):
+            flat = sum(sums[v, f, :, k : k + LANES] for k in range(0, d.degrees, LANES))
+            norms[0, 4 * v + f : 4 * v + f + 1, :] = jnp.sum(flat, axis=0, keepdims=True)
+    norms[1] = spread("band", band, n, band_norms, 0)
+    total_out[...] = spread("node", node, d.nnode, node_norms, 1)
+
+
+def sweep(d, iterate, legendre, state, rate, trig, cor, weight, quadrature):
+    anywhere, vmem = pl.BlockSpec(memory_space=pl.ANY), pl.BlockSpec(memory_space=pltpu.VMEM)
+    line = pltpu.VMEM((d.nc, d.mc, d.rows, d.degrees), BF16)
+    dma = pltpu.SemaphoreType.DMA
+    back = (d.el - 1) * d.fields + d.nc
+    per = d.mc // 2
+    return pl.pallas_call(
+        functools.partial(sweep_kernel, d),
+        name="sweep",
+        out_shape=(
+            jax.ShapeDtypeStruct(iterate.shape, F32),
+            jax.ShapeDtypeStruct((8, LANES), F32),
+            jax.ShapeDtypeStruct((d.el * d.g, d.n, d.pl, 2 * d.lb), BF16),
+            jax.ShapeDtypeStruct((d.el, d.n, d.g, d.pl, 2 * d.lb), BF16),
+        ),
+        in_specs=[anywhere] * 4 + [vmem] * 3 + [pl.BlockSpec(memory_space=pltpu.SMEM)],
+        out_specs=(anywhere, vmem, anywhere, anywhere),
+        scratch_shapes=[
+            pltpu.VMEM((d.nc, d.el, d.n, d.g, per, 2 * d.lb), BF16),
+            pltpu.VMEM((2, 2, 3, 4 * d.kc, d.half), BF16),
+            pltpu.VMEM((2, 2, 2 * d.half, d.half), BF16),
+            pltpu.VMEM((d.el * d.g, d.half, 2 * d.lb), BF16),
+            line,
+            line,
+            line,
+            pltpu.VMEM((2, d.fields, d.members, d.degrees), F32),
+            pltpu.VMEM((2, 8, LANES), F32),
+            pltpu.VMEM((d.n, 8, LANES), F32),
+            pltpu.VMEM((d.nnode, 8, LANES), F32),
+            dma((2, 4)),
+            dma((d.el * d.nc, d.n)),
+            dma((d.el * d.nc, d.n)),
+            dma((d.el * d.nc,)),
+            dma((1,)),
+            dma((back, d.n)),
+            dma((back, d.n)),
+            dma((back,)),
+            dma((2,)),
+            dma((d.nc,)),
+            dma((d.nc,)),
+            dma((d.nc,)),
+            dma((d.nc,)),
+            dma((d.nc,)),
+            dma((d.nc,)),
+            dma((2, 3)),
+            dma((2,)),
+            dma((2, 2, d.n)),
+        ],
+        compiler_params=pltpu.CompilerParams(
+            collective_id=1, has_side_effects=True, vmem_limit_bytes=VMEM_BYTES
+        ),
+    )(iterate, legendre, state, rate, trig, cor, weight, quadrature)
+
+
+def fast_body(d, state0, iterate, legendre, lat_weight, coriolis, damping, quadrature):
+    band = lax.axis_index("band")
+    first = (band // d.eg) * d.lb
+    cor = lax.dynamic_slice_in_dim(coriolis, first, d.lb, 1)
+    weight = jnp.tile(lax.dynamic_slice_in_dim(lat_weight, first, d.lb, 0), 2)[None]
+    iterate, state0 = jnp.swapaxes(iterate, 3, 4), jnp.swapaxes(state0, 2, 3)
+    damping = jnp.swapaxes(damping, 0, 1)
+    trig = jnp.asarray(trig_rows(d))
+    updated, norms, _, _ = sweep(d, iterate, legendre, state0, damping, trig, cor, weight, quadrature)
+    total = norms.reshape(2, 4, LANES)[:, : d.fields].sum(axis=2)
+    return jnp.swapaxes(updated, 3, 4), jnp.sqrt(total[0] / (total[1] + 1e-06))
+
+
 def solution(mesh):
     placed = (
         P(None, "band", None, None, None),
@@ -154,10 +888,16 @@
         P("band", None, None),
         P(),
     )
-    return jax.shard_map(
-        body,
-        mesh=mesh,
-        in_specs=placed,
-        out_specs=(P("node", None, "band", None, None, None), P()),
-        check_vma=False,
-    )
+
+    def call(*args):
+        d = Plan(mesh.shape["band"], mesh.shape["node"], args[1].shape, args[2].shape)
+        body = functools.partial(fast_body, d) if d.fits else plain_body
+        return jax.shard_map(
+            body,
+            mesh=mesh,
+            in_specs=placed,
+            out_specs=(P("node", None, "band", None, None, None), P()),
+            check_vma=False,
+        )(*args)
+
+    return call

time: 781 us -> 306 us (0.39); the launches traced: 770 us -> 305 us
  Pallas kernels: 0 us -> 294 us
  waiting for transfers between devices: 239 us -> 0 us
  local copies, waits for them, and re-layouts: 212 us -> 8.49 us
  matrix products: 173 us -> 0 us
  other arithmetic: 72.5 us -> 1.29 us
  blocking collectives: 38.3 us -> 0 us
  starting transfers between devices: 19.7 us -> 0 us
  between operations: 15.3 us -> 0.67 us
    pallas_call x0 -> x1, Pallas kernels: none -> 294 us  [sweep(): pl.pallas_call(functools.partial(sweep_kernel, d), name='sweep', out_shap...]
    all_gather x2 -> x0, waiting for transfers between devices: 217 us -> none  [analysis(): gathered = lax.all_gather(rest.astype(jnp.bfloat16), 'node')]
    dot_general x32 -> x0, matrix products: 173 us -> none  [the longest x28 67.6 us: mul(): lax.dot_general(a, b, (dims, ((), ())), preferred_element_type=jnp.float32)]
    reshape x16 -> x0, local copies, waits for them, and re-layouts: 153 us -> none  [the longest x4 49.5 us: analysis(): out = out.reshape(nband, 2, 2, pairs, 2, fields, ens, lat_rows)]
    psum x1 -> x0, blocking collectives: 38.3 us -> none  [body(): total = lax.psum(jnp.stack([change, base]), ('node', 'band'))]
    slice x5 -> x0, local copies, waits for them, and re-layouts: 22.2 us -> none  [the longest x2 14.5 us: analysis(): both[:, 0]]
    add x17 -> x0, other arithmetic: 21.6 us -> none  [the longest x2 13.3 us: analysis(): sum((quad_row[p] * gathered[p].astype(jnp.float32) for p in range(nnode)))]
    all_to_all x4 -> x0, waiting for transfers between devices: 20.7 us -> none  [the longest x2 15.6 us: synthesis(): return lax.all_to_all(four, 'band', split_axis=0, concat_axis=0, tiled=True)]
  transfers between devices with their start and end apart: 6 -> 0, of which waited for: 4 -> 0; matrix products, arithmetic and copies ran while one was open for 28% -> 0% of each run, Pallas kernels for 0% -> 0%
where the time goes in v2:
time: 306 us; the launch traced here: 305 us
  Pallas kernels  294 us (96%)
  local copies, waits for them, and re-layouts  8.49 us (3%)
    pallas_call x1, Pallas kernels, sweep(): pl.pallas_call(functools.partial(sweep_kernel, d), name='sweep', out_shap...  294 us
    unnamed x3, local copies, waits for them, and re-layouts  6.57 us

profile of v2, /device:TPU:0, one launch (start us, length us, event | category | flops | bytes accessed | tf_op | source)
XLA Modules:
  0.0 304.9 jit_solution(10010347392551806049)
XLA Ops:
  0.6 0.0 copy-start
  0.7 0.8 dynamic_slice.7
  1.4 0.0 copy-done
  1.4 0.6 constant_dynamic-slice_fusion.cor
  2.0 0.6 tile.2
  2.6 294.5 %sweep.1 = (f32[1,2,128,3,4,512]{5,4,3,2,1,0:T(4,128)}, f32[8,128]{1,0:T(8,128)}, bf16[24,8,64,256]{3,2,1,0:T(8,128)(2,1)}, bf16[2,8,12,64,256]{4,3,2,1,0:T(8,128)(2,1)}) custom-call(f32[1,2,128,3,4,512]{5,4,3,2,1,0:T(4,128)} %bitcast.8, bf16[128,512,512]{2,1,0:T(8,128)(2,1)} %leg_hbm.1, f32[2,128,3,4,512]{4,3,2,1,0:T(4,128)} %bitcast.9, ...), custom_call_target="tpu_custom_call" | custom-call | tf_op jit(solution)/shard_map/sweep/pallas_call | solution.py:820
  297.1 0.8 slice_reduce_fusion
  297.8 0.5 sqrt_bitcast_fusion
  298.4 6.6 %copy.11 = f32[1,2,128,4,3,512]{5,3,4,2,1,0:T(4,128)} copy(f32[1,2,128,4,3,512]{5,3,4,2,1,0:T(4,128)} %bitcast.10) | data formatting | bytes 12582912
Async XLA Ops:
  0.6 0.8 copy-start

commit v3 on v2

--- a/solution.py
+++ b/solution.py
@@ -163,8 +163,10 @@
         self.lb = LANES
         self.nlb = self.hemi // self.lb
         self.eg = max(nband // max(self.nlb, 1), 1)
-        self.el = self.members // self.eg
-        self.rows = 2 * self.members * self.fields
+        self.items = nnode
+        self.el = self.items // self.eg
+        self.k = 2 * self.fields
+        self.rows = self.items * self.k
         self.pl = self.ml // 2
         self.mc = 16
         self.nc = self.ml // self.mc
@@ -175,7 +177,8 @@
             nnode == 4
             and self.fields == 3
             and self.nlb * self.eg == nband
-            and self.eg * self.el == self.members
+            and self.members == nnode
+            and self.eg * self.el == self.items
             and self.hemi % self.lb == 0
             and self.ml % self.mc == 0
             and self.modes % nband == 0
@@ -185,14 +188,7 @@
         )
 
 
-def gather_rows(d, rows, piece):
-    for cc in range(2):
-        for f in range(d.fields):
-            r = (cc * d.fields + f) * d.members
-            rows[r : r + d.members, :] = piece(cc, f)
-
-
-def build_tables(d, trig, fwd, back):
+def build_tables(d, trig, fwd, back, step):
     tall, fine = 3 * d.kc // 16, 16
     short = d.half // 16
 
@@ -218,7 +214,7 @@
                     ).astype(BF16)
             return _
 
-        lax.fori_loop(0, tall, ahead, None)
+        lax.fori_loop(step * tall // d.nc, (step + 1) * tall // d.nc, ahead, None)
         first = jnp.where(lax.broadcasted_iota(jnp.int32, (1, d.half), 1) == 0, 0.5, 1.0)
 
         def behind(a, _):
@@ -231,7 +227,7 @@
                 back[p, cc, pl.ds(pl.multiple_of(d.half + at, 16), 16)] = (t - top.astype(F32)).astype(BF16)
             return _
 
-        lax.fori_loop(0, short, behind, None)
+        lax.fori_loop(step * short // d.nc, (step + 1) * short // d.nc, behind, None)
 
 
 def trig_rows(d):
@@ -248,6 +244,17 @@
     return np.stack([np.cos(angle) * scale, np.sin(angle) * scale]).astype(np.float32)
 
 
+def encode(x):
+    y = x * 2.0**-9
+    return (y * y * y).astype(BF16)
+
+
+def decode(y):
+    y = y.astype(F32)
+    root = jnp.exp2(jnp.log2(jnp.maximum(jnp.abs(y), 2.0**-126)) * (1.0 / 3.0)) * 2.0**9
+    return jnp.where(y == 0.0, 0.0, jnp.where(y < 0.0, -root, root))
+
+
 def four_points(ce, se, co, so):
     a, b, c, e = ce + se, ce - se, co + so, co - so
     return a + c, b + e, a - c, b - e
@@ -261,9 +268,9 @@
 def sweep_kernel(
     d, it_hbm, leg_hbm, state_hbm, rate_hbm, trig, cor, weight, quad,
     out, total_out, x_hbm, spectra,
-    send, fwd, back, send_back, outer, cross, far, sums, norms, band_norms, node_norms,
-    leg_sem, a_send, a_recv, a_own, x_sem, b_send, b_recv, b_own, recv_sem,
-    own_send, fwd_send, par_send, o_sem, x_recv, y_sem, buf_sem, res_sem, norm_sem,
+    send, fwd, back, send_back, ready, coeff, mixed_in, own_low, sums, norms, band_norms, node_norms,
+    leg_sem, c_send, c_recv, a_send, a_recv, a_own, x_sem, b_send, b_recv, b_own, recv_sem,
+    m_send, m_recv, buf_sem, res_sem, norm_sem,
 ):
     band, node = lax.axis_index("band"), lax.axis_index("node")
     n, g, half = d.n, d.g, d.degrees // 2
@@ -277,6 +284,64 @@
     for axis, peer in near:
         pl.semaphore_signal(sem, inc=1, device_id={axis: peer}, device_id_type=MESH)
     pl.semaphore_wait(sem, len(near))
+
+    def give(c, off):
+        peer = lax.rem(node + off, d.nnode)
+        return pltpu.make_async_remote_copy(
+            src_ref=ready.at[c, peer],
+            dst_ref=coeff.at[c, node],
+            send_sem=c_send.at[c, off],
+            recv_sem=c_recv.at[c, off],
+            device_id={"node": peer},
+            device_id_type=MESH,
+        )
+
+    width = d.k * d.mc
+
+    def hand_out(raw, rows):
+        def fetch(c, slot):
+            return pltpu.make_async_copy(it_hbm.at[0, :, pl.ds(c * d.mc, d.mc)], raw.at[slot], leg_sem.at[slot, 0])
+
+        fetch(0, 0).start()
+
+        def chunk(c, _):
+            slot = lax.rem(c, 2)
+
+            @pl.when(c + 1 < d.nc)
+            def _():
+                fetch(c + 1, 1 - slot).start()
+
+            fetch(c, slot).wait()
+
+            def mode(m, _):
+                for cc in range(2):
+                    for f in range(d.fields):
+                        y = raw[slot, cc, m, f]
+                        for t in range(d.degrees // LANES):
+                            rows[t, pl.ds((cc * d.fields + f) * d.mc + m, d.members, stride=width), :] = y[
+                                :, t * LANES : (t + 1) * LANES
+                            ]
+                return _
+
+            lax.fori_loop(0, d.mc, mode, None)
+            for t in range(d.degrees // LANES):
+                cols = slice(t * LANES, (t + 1) * LANES)
+                for e in range(d.members):
+                    ready[c, e, :, cols] = rows[t, e * width : (e + 1) * width].astype(BF16)
+                mine = rows[t, pl.ds(pl.multiple_of(node * width, width), width)]
+                own_low[c, :, cols] = (mine - mine.astype(BF16).astype(F32)).astype(BF16)
+            coeff[c, node] = ready[c, node]
+            for off in range(1, d.nnode):
+                give(c, off).start()
+            return _
+
+        lax.fori_loop(0, d.nc, chunk, None)
+
+    pl.run_scoped(
+        hand_out,
+        pltpu.VMEM((2, 2, d.mc, d.fields, d.members, d.degrees), F32),
+        pltpu.VMEM((d.degrees // LANES, d.members * width, LANES), F32),
+    )
 
     def ahead(s, c, off):
         peer = lax.rem(band + off, n)
@@ -299,32 +364,34 @@
             ahead(s, c, off).start()
         ahead_own(s, c).start()
 
-    def synthesis(raw, rows, leg, stage):
+    def synthesis(rows, leg, stage):
         def fetch(i, slot):
-            return [
-                pltpu.make_async_copy(leg_hbm.at[pl.ds(i * SUB, SUB)], leg.at[slot], leg_sem.at[slot, 0]),
-                pltpu.make_async_copy(it_hbm.at[0, :, pl.ds(i * SUB, SUB)], raw.at[slot], leg_sem.at[slot, 1]),
-            ]
-
-        for copy_in in fetch(0, 0):
-            copy_in.start()
+            return pltpu.make_async_copy(leg_hbm.at[pl.ds(i * SUB, SUB)], leg.at[slot], leg_sem.at[slot, 0])
+
+        fetch(0, 0).start()
 
         def chunk(c, _):
+            build_tables(d, trig, fwd, back, c)
+            for off in range(1, d.nnode):
+                give(c, off).wait_recv()
+            for p in range(d.items):
+                for t in range(d.degrees // LANES):
+                    rows[t, p * width : (p + 1) * width] = coeff[c, p, :, t * LANES : (t + 1) * LANES].astype(F32)
+
             def sub(j, _):
                 i = c * subs + j
                 slot = lax.rem(i, 2)
 
                 @pl.when(i + 1 < total)
                 def _():
-                    for copy_in in fetch(i + 1, 1 - slot):
-                        copy_in.start()
-
-                for copy_in in fetch(i, slot):
-                    copy_in.wait()
+                    fetch(i + 1, 1 - slot).start()
+
+                fetch(i, slot).wait()
                 for mi in range(SUB):
-                    gather_rows(d, rows.at[mi], lambda cc, f: raw[slot, cc, mi, f])
-                for mi in range(SUB):
-                    x = rows[mi].astype(BF16)
+                    pieces = [
+                        rows[t, pl.ds(j * SUB + mi, d.rows, stride=d.mc), :] for t in range(d.degrees // LANES)
+                    ]
+                    x = jnp.concatenate(pieces, axis=1).astype(BF16)
                     table = leg[slot, mi]
                     for par in range(2):
                         cols = slice(par * half, (par + 1) * half)
@@ -341,7 +408,7 @@
                         for cc in range(2):
                             for lb in range(d.nlb):
                                 for eg in range(d.eg):
-                                    r = (cc * d.fields + f) * d.members + eg * d.el + s
+                                    r = ((eg * d.el + s) * 2 + cc) * d.fields + f
                                     tiles = [
                                         stage[pl.ds(((lb * 2 + par) * d.rows + r) * d.mc + p * per, per), :]
                                         for par in range(2)
@@ -349,26 +416,18 @@
                                     send[c, s, lb * d.eg + eg, (f * 2 + p) * 2 + cc] = jnp.concatenate(
                                         tiles, axis=1
                                     ).astype(BF16)
-            start_ahead(0, c)
+            for s in range(d.el):
+                start_ahead(s, c)
             return _
 
         lax.fori_loop(0, d.nc, chunk, None)
 
     pl.run_scoped(
         synthesis,
-        pltpu.VMEM((2, 2, SUB, d.fields, d.members, d.degrees), F32),
-        pltpu.VMEM((SUB, d.rows, d.degrees), F32),
+        pltpu.VMEM((d.degrees // LANES, d.rows * d.mc, LANES), F32),
         pltpu.VMEM((2, SUB, d.hemi, d.degrees), BF16),
         pltpu.VMEM((2 * d.nlb * d.rows * d.mc, LANES), F32),
     )
-    if d.el > 1:
-
-        def rest(i, _):
-            start_ahead(1 + i // d.nc, lax.rem(i, d.nc))
-            return _
-
-        lax.fori_loop(0, last * d.nc, rest, None)
-    build_tables(d, trig, fwd, back)
 
     def behind(s, f, off):
         peer = lax.rem(band + off, n)
@@ -518,38 +577,29 @@
         pltpu.VMEM((g, 8, 2 * d.lb), F32),
     )
 
-    is_outer = lax.rem(node, 3) == 0
-    is_inner = jnp.logical_not(is_outer)
-    beside = jnp.where(is_outer, 1 + node // 3, (node - 1) * 3)
-    other = jnp.where(is_outer, beside, 3 - node)
-    far_node = jnp.where(is_outer, 0, 3 - beside)
-
-    def analysis(leg, raw, damp, drift, recv, lhs, own, partial, bufs, rates, mix_rows, result):
-        def copy(src, dst, send_s, recv_s, c, peer):
-            return pltpu.make_async_remote_copy(
-                src_ref=src.at[c], dst_ref=dst.at[c], send_sem=send_s.at[c], recv_sem=recv_s.at[c],
-                device_id={"node": peer}, device_id_type=MESH,
-            )
-
-        def to_inner(c):
-            return copy(own, outer, own_send, o_sem, c, beside)
-
-        def to_other(c):
-            return copy(own, cross, own_send, x_recv, c, other)
-
-        def forward(c):
-            return copy(outer, far, fwd_send, y_sem, c, other)
-
-        def to_outer(c):
-            return copy(partial, cross, par_send, x_recv, c, beside)
+    def home(c, off):
+        peer = lax.rem(node + off, d.nnode)
+        return pltpu.make_async_remote_copy(
+            src_ref=ready.at[c, peer],
+            dst_ref=mixed_in.at[c, node],
+            send_sem=m_send.at[c, off],
+            recv_sem=m_recv.at[c, off],
+            device_id={"node": peer},
+            device_id_type=MESH,
+        )
+
+    def analysis(leg, state_in, damp, recv, lhs, mix, bufs, rates, mix_rows, result):
+        tiles = d.degrees // LANES
+        tall = 8 * d.mc
 
         def fetch(i, slot):
-            at = pl.ds(i * SUB, SUB)
+            return pltpu.make_async_copy(leg_hbm.at[pl.ds(i * SUB, SUB)], leg.at[slot], leg_sem.at[slot, 0])
+
+        def fetch_linear(c, slot):
+            at = pl.ds(c * d.mc, d.mc)
             return [
-                pltpu.make_async_copy(leg_hbm.at[at], leg.at[slot], leg_sem.at[slot, 0]),
-                pltpu.make_async_copy(it_hbm.at[0, :, at], raw.at[slot, 0], leg_sem.at[slot, 1]),
-                pltpu.make_async_copy(state_hbm.at[:, at], raw.at[slot, 1], leg_sem.at[slot, 2]),
-                pltpu.make_async_copy(rate_hbm.at[:, at], damp.at[slot], leg_sem.at[slot, 3]),
+                pltpu.make_async_copy(state_hbm.at[:, at], state_in.at[slot], leg_sem.at[slot, 1]),
+                pltpu.make_async_copy(rate_hbm.at[:, at], damp.at[slot], leg_sem.at[slot, 2]),
             ]
 
         def fetch_spectra(c, slot):
@@ -562,8 +612,16 @@
                 final(c, off).wait_recv()
             final_own(c).wait()
 
-        for copy_in in fetch(0, 0):
+        fetch(0, 0).start()
+        for copy_in in fetch_linear(0, 0):
             copy_in.start()
+
+        def freed(c, _):
+            for off in range(1, d.nnode):
+                give(c, off).wait_send()
+            return _
+
+        lax.fori_loop(0, d.nc, freed, None)
 
         def early(i, _):
             s, f = i // d.fields, lax.rem(i, d.fields)
@@ -585,7 +643,7 @@
                         for f in range(d.fields):
                             for p in range(2):
                                 for cc in range(2):
-                                    r = (cc * d.fields + f) * d.members + eg * d.el + s
+                                    r = ((eg * d.el + s) * 2 + cc) * d.fields + f
                                     tile = recv[cslot, s, lb * d.eg + eg, f * 4 + p * 2 + cc].astype(F32)
                                     for par in range(2):
                                         at = ((par * d.nlb + lb) * d.rows + r) * d.mc + p * per
@@ -597,50 +655,63 @@
 
                 @pl.when(i + 1 < total)
                 def _():
-                    for copy_in in fetch(i + 1, 1 - slot):
-                        copy_in.start()
-
-                for copy_in in fetch(i, slot):
-                    copy_in.wait()
-                for mi in range(SUB):
-                    gather_rows(
-                        d,
-                        drift.at[mi],
-                        lambda cc, f: damp[slot, f, mi : mi + 1] * (raw[slot, 0, cc, mi, f] - raw[slot, 1, cc, mi, f]),
-                    )
+                    fetch(i + 1, 1 - slot).start()
+
+                fetch(i, slot).wait()
                 for mi in range(SUB):
                     for par in range(2):
-                        pieces = [
-                            lhs[
-                                pl.ds(
-                                    (par * d.nlb + lb) * d.rows * d.mc + (mi % 2) * per + j * (SUB // 2) + mi // 2,
-                                    d.rows,
-                                    stride=d.mc,
-                                ),
-                                :,
-                            ]
-                            for lb in range(d.nlb)
-                        ]
-                        rows = jnp.concatenate(pieces, axis=1).astype(BF16)
-                        cols = slice(par * half, (par + 1) * half)
-                        y = mul(rows, leg[slot, mi, :, cols], ((1,), (0,)))
-                        own[c, j * SUB + mi, :, cols] = (y - drift[mi, :, cols]).astype(BF16)
+                        pieces = []
+                        for lb in range(d.nlb):
+                            at = (par * d.nlb + lb) * d.rows * d.mc + (mi % 2) * per + j * (SUB // 2) + mi // 2
+                            pieces.append(
+                                jnp.concatenate(
+                                    [lhs[pl.ds(at + p * width, 8, stride=d.mc), :] for p in range(d.items)], axis=0
+                                )
+                            )
+                        x = jnp.concatenate(pieces, axis=1).astype(BF16)
+                        y = mul(x, leg[slot, mi, :, par * half : (par + 1) * half], ((1,), (0,)))
+                        y = [y[8 * p : 8 * p + 8] for p in range(d.items)]
+                        for q in range(d.nnode):
+                            z = sum(quad[q, p] * y[p] for p in range(d.items))
+                            for t in range(tiles // 2):
+                                mix[par * (tiles // 2) + t, pl.ds(q * tall + j * SUB + mi, 8, stride=d.mc), :] = z[
+                                    :, t * LANES : (t + 1) * LANES
+                                ]
                 return _
 
             lax.fori_loop(0, subs, sub, None)
 
-            @pl.when(is_outer)
+            @pl.when(c + 1 < d.nc)
             def _():
-                to_inner(c).start()
-
-            @pl.when(is_inner)
-            def _():
-                to_other(c).start()
-
-                @pl.when(c >= 1)
-                def _():
-                    to_inner(c - 1).wait_recv()
-                    forward(c - 1).start()
+                for copy_in in fetch_linear(c + 1, 1 - cslot):
+                    copy_in.start()
+
+            for copy_in in fetch_linear(c, cslot):
+                copy_in.wait()
+
+            def linear(k, _):
+                cc = k // d.fields
+                f = k - cc * d.fields
+                at = pl.multiple_of(k * d.mc, d.mc)
+                start = state_in[cslot, cc, :, f, pl.ds(node, 1), :].reshape(d.mc, d.degrees)
+                rate = damp[cslot, f]
+                low = own_low[c, pl.ds(at, d.mc)].astype(F32)
+                pull = []
+                for p in range(d.items):
+                    spec = coeff[c, p, pl.ds(at, d.mc)].astype(F32) + jnp.where(node == p, low, 0.0)
+                    pull.append(rate * (spec - start))
+                for q in range(d.nnode):
+                    away = sum(quad[q, p] * pull[p] for p in range(d.items) if p != q)
+                    for t in range(tiles):
+                        cols = slice(t * LANES, (t + 1) * LANES)
+                        z = mix[t, pl.ds(pl.multiple_of(q * tall + k * d.mc, d.mc), d.mc), :]
+                        ready[c, q, pl.ds(at, d.mc), cols] = encode(z - away[:, cols])
+                return _
+
+            lax.fori_loop(0, d.k, linear, None)
+            mixed_in[c, node] = ready[c, node]
+            for off in range(1, d.nnode):
+                home(c, off).start()
 
             @pl.when(c + 1 < d.nc)
             def _():
@@ -650,11 +721,6 @@
             return _
 
         lax.fori_loop(0, d.nc, chunk, None)
-
-        @pl.when(is_inner)
-        def _():
-            to_inner(d.nc - 1).wait_recv()
-            forward(d.nc - 1).start()
 
         def load(c, slot):
             at = pl.ds(c * d.mc, d.mc)
@@ -688,46 +754,27 @@
             def _():
                 save(c - 2, slot).wait()
 
-            @pl.when(is_inner)
-            def _():
-                to_other(c).wait_recv()
-                forward(c).wait_recv()
-
-                def mode(m, _):
-                    a, b = own[c, m].astype(F32), cross[c, m].astype(F32)
-                    o, y = outer[c, m].astype(F32), far[c, m].astype(F32)
-                    mix = quad[beside, node] * a + quad[beside, other] * b + quad[beside, far_node] * y
-                    partial[c, m] = mix.astype(BF16)
-                    mix_rows[m] = (
-                        q_own * a + quad[node, other] * b + quad[node, beside] * o + quad[node, far_node] * y
-                    )
-                    return _
-
-                lax.fori_loop(0, d.mc, mode, None)
-                to_outer(c).start()
-
-            @pl.when(is_outer)
-            def _():
-                to_outer(c).wait_recv()
-
-                def mode(m, _):
-                    mix_rows[m] = q_own * own[c, m].astype(F32) + cross[c, m].astype(F32)
-                    return _
-
-                lax.fori_loop(0, d.mc, mode, None)
+            for off in range(1, d.nnode):
+                home(c, off).wait_recv()
+            for e in range(d.members):
+                for t in range(tiles):
+                    mix_rows[t, e * width : (e + 1) * width] = decode(mixed_in[c, e, :, t * LANES : (t + 1) * LANES])
 
             def update(m, _):
                 for f in range(d.fields):
                     rate = rates[slot, f, pl.ds(m, 1)]
                     scale = q_own * rate
                     below = 1.0 + scale
-                    pull = q_total * rate
+                    pull = (q_total - q_own) * rate
                     changed, start = sums[0, f], sums[1, f]
                     for cc in range(2):
-                        r = (cc * d.fields + f) * d.members
                         state, spec = bufs[slot, 0, cc, m, f], bufs[slot, 1, cc, m, f]
-                        mixed = mix_rows[m, r : r + d.members, :] - pull * state
-                        new = (state + mixed + scale * spec) / below
+                        at = (cc * d.fields + f) * d.mc + m
+                        mixed = jnp.concatenate(
+                            [mix_rows[t, pl.ds(at, d.members, stride=width), :] for t in range(tiles)], axis=1
+                        )
+                        force = mixed - pull * state - scale * spec
+                        new = (state + force + scale * spec) / below
                         result[slot, cc, m, f] = new
                         changed += (new - spec) * (new - spec)
                         start += state * state
@@ -744,16 +791,8 @@
             save(c, c % 2).wait()
 
         def finish(c, _):
-            @pl.when(is_outer)
-            def _():
-                to_inner(c).wait_send()
-
-            @pl.when(is_inner)
-            def _():
-                to_other(c).wait_send()
-                forward(c).wait_send()
-                to_outer(c).wait_send()
-
+            for off in range(1, d.nnode):
+                home(c, off).wait_send()
             for off in range(1, n):
                 final(c, off).wait_send()
                 for s in range(d.el):
@@ -773,16 +812,14 @@
     pl.run_scoped(
         analysis,
         pltpu.VMEM((2, SUB, d.hemi, d.degrees), BF16),
-        pltpu.VMEM((2, 2, 2, SUB, d.fields, d.members, d.degrees), F32),
-        pltpu.VMEM((2, d.fields, SUB, d.degrees), F32),
-        pltpu.VMEM((SUB, d.rows, d.degrees), F32),
+        pltpu.VMEM((2,) + natural, F32),
+        pltpu.VMEM((2, d.fields, d.mc, d.degrees), F32),
         pltpu.VMEM((2, d.el, n, g, per, 2 * d.lb), BF16),
-        pltpu.VMEM((2 * d.nlb * d.rows * d.mc, LANES), F32),
-        pltpu.VMEM((d.nc, d.mc, d.rows, d.degrees), BF16),
-        pltpu.VMEM((d.nc, d.mc, d.rows, d.degrees), BF16),
+        pltpu.VMEM((2 * d.nlb * d.rows * d.mc + 2 * d.mc, LANES), F32),
+        pltpu.VMEM((d.degrees // LANES, d.nnode * 8 * d.mc, LANES), F32),
         pltpu.VMEM((2, 2) + natural, F32),
         pltpu.VMEM((2, d.fields, d.mc, d.degrees), F32),
-        pltpu.VMEM((d.mc, d.rows, d.degrees), F32),
+        pltpu.VMEM((d.degrees // LANES, d.members * width, LANES), F32),
         pltpu.VMEM((2,) + natural, F32),
     )
 
@@ -813,7 +850,7 @@
 
 def sweep(d, iterate, legendre, state, rate, trig, cor, weight, quadrature):
     anywhere, vmem = pl.BlockSpec(memory_space=pl.ANY), pl.BlockSpec(memory_space=pltpu.VMEM)
-    line = pltpu.VMEM((d.nc, d.mc, d.rows, d.degrees), BF16)
+    line = pltpu.VMEM((d.nc, d.nnode, d.k * d.mc, d.degrees), BF16)
     dma = pltpu.SemaphoreType.DMA
     back = (d.el - 1) * d.fields + d.nc
     per = d.mc // 2
@@ -836,11 +873,14 @@
             line,
             line,
             line,
+            pltpu.VMEM((d.nc, d.k * d.mc, d.degrees), BF16),
             pltpu.VMEM((2, d.fields, d.members, d.degrees), F32),
             pltpu.VMEM((2, 8, LANES), F32),
             pltpu.VMEM((d.n, 8, LANES), F32),
             pltpu.VMEM((d.nnode, 8, LANES), F32),
-            dma((2, 4)),
+            dma((2, 3)),
+            dma((d.nc, d.nnode)),
+            dma((d.nc, d.nnode)),
             dma((d.el * d.nc, d.n)),
             dma((d.el * d.nc, d.n)),
             dma((d.el * d.nc,)),
@@ -849,12 +889,8 @@
             dma((back, d.n)),
             dma((back,)),
             dma((2,)),
-            dma((d.nc,)),
-            dma((d.nc,)),
-            dma((d.nc,)),
-            dma((d.nc,)),
-            dma((d.nc,)),
-            dma((d.nc,)),
+            dma((d.nc, d.nnode)),
+            dma((d.nc, d.nnode)),
             dma((2, 3)),
             dma((2,)),
             dma((2, 2, d.n)),

time: 306 us -> 263 us (0.86)
  Pallas kernels: 294 us -> 251 us
    pallas_call x1, Pallas kernels: 294 us -> 251 us  [sweep(): pl.pallas_call(functools.partial(sweep_kernel, d), name='sweep', out_shap...]
where the time goes in v3:
time: 263 us; the launch traced here: 262 us
  Pallas kernels  251 us (95%)
  local copies, waits for them, and re-layouts  8.49 us (3%)
    pallas_call x1, Pallas kernels, sweep(): pl.pallas_call(functools.partial(sweep_kernel, d), name='sweep', out_shap...  251 us
    unnamed x3, local copies, waits for them, and re-layouts  6.57 us

profile of v3, /device:TPU:0, one launch (start us, length us, event | category | flops | bytes accessed | tf_op | source)
XLA Modules:
  0.0 261.6 jit_solution(2593446002932189595)
XLA Ops:
  0.6 0.0 copy-start
  0.7 0.8 dynamic_slice.7
  1.4 0.0 copy-done
  1.4 0.6 constant_dynamic-slice_fusion.cor
  2.0 0.6 tile.2
  2.6 251.1 %sweep.1 = (f32[1,2,128,3,4,512]{5,4,3,2,1,0:T(4,128)}, f32[8,128]{1,0:T(8,128)}, bf16[24,8,64,256]{3,2,1,0:T(8,128)(2,1)}, bf16[2,8,12,64,256]{4,3,2,1,0:T(8,128)(2,1)}) custom-call(f32[1,2,128,3,4,512]{5,4,3,2,1,0:T(4,128)} %bitcast.8, bf16[128,512,512]{2,1,0:T(8,128)(2,1)} %leg_hbm.1, f32[2,128,3,4,512]{4,3,2,1,0:T(4,128)} %bitcast.9, ...), custom_call_target="tpu_custom_call" | custom-call | tf_op jit(solution)/shard_map/sweep/pallas_call | solution.py:857
  253.7 0.8 slice_reduce_fusion
  254.5 0.5 sqrt_bitcast_fusion
  255.0 6.6 %copy.11 = f32[1,2,128,4,3,512]{5,3,4,2,1,0:T(4,128)} copy(f32[1,2,128,4,3,512]{5,3,4,2,1,0:T(4,128)} %bitcast.10) | data formatting | bytes 12582912
Async XLA Ops:
  0.6 0.8 copy-start

commit v4 on v3

--- a/solution.py
+++ b/solution.py
@@ -13,7 +13,7 @@
 F32, BF16 = jnp.float32, jnp.bfloat16
 VMEM_BYTES = 63_000_000
 LANES = 128
-SUB = 4
+SUB = 8
 
 
 def split_bf16(x):
@@ -470,7 +470,10 @@
     def grid(x, part, high, low, edge):
         kc, lb = d.kc, d.lb
 
-        def step(s, _):
+        def fetch(s):
+            return pltpu.make_async_copy(x_hbm.at[pl.ds(s * g, g)], x, x_sem.at[0])
+
+        def begin(s):
             def arrive(c, _):
                 for off in range(1, n):
                     ahead(s, c, off).wait_recv()
@@ -478,9 +481,12 @@
                 return _
 
             lax.fori_loop(0, d.nc, arrive, None)
-            fetch = pltpu.make_async_copy(x_hbm.at[pl.ds(s * g, g)], x, x_sem.at[0])
-            fetch.start()
-            fetch.wait()
+            fetch(s).start()
+
+        begin(0)
+
+        def step(s, _):
+            fetch(s).wait()
 
             def rows(c, _):
                 def field(f, _):
@@ -535,6 +541,10 @@
 
             lax.fori_loop(0, 3, rows, None)
 
+            @pl.when(s < last)
+            def _():
+                begin(s + 1)
+
             def field(f, _):
                 for q in range(4):
                     p, cc = divmod(q, 2)
@@ -787,6 +797,30 @@
             return _
 
         lax.fori_loop(0, d.nc, combine, None)
+        def spread(axis, me, count, slots, k):
+            slots[me] = norms[k]
+            copies = [
+                pltpu.make_async_remote_copy(
+                    src_ref=norms.at[k], dst_ref=slots.at[me],
+                    send_sem=norm_sem.at[k, 0, off], recv_sem=norm_sem.at[k, 1, off],
+                    device_id={axis: lax.rem(me + off, count)}, device_id_type=MESH,
+                )
+                for off in range(1, count)
+            ]
+            for each in copies:
+                each.start()
+            for each in copies:
+                each.wait()
+            return sum(slots[i] for i in range(count))
+
+        norms[...] = jnp.zeros_like(norms)
+        for v in range(2):
+            for f in range(d.fields):
+                flat = sum(sums[v, f, :, k : k + LANES] for k in range(0, d.degrees, LANES))
+                norms[0, 4 * v + f : 4 * v + f + 1, :] = jnp.sum(flat, axis=0, keepdims=True)
+        norms[1] = spread("band", band, n, band_norms, 0)
+        total_out[...] = spread("node", node, d.nnode, node_norms, 1)
+
         for c in range(max(d.nc - 2, 0), d.nc):
             save(c, c % 2).wait()
 
@@ -822,30 +856,6 @@
         pltpu.VMEM((d.degrees // LANES, d.members * width, LANES), F32),
         pltpu.VMEM((2,) + natural, F32),
     )
-
-    def spread(axis, me, count, slots, k):
-        slots[me] = norms[k]
-        copies = [
-            pltpu.make_async_remote_copy(
-                src_ref=norms.at[k], dst_ref=slots.at[me],
-                send_sem=norm_sem.at[k, 0, off], recv_sem=norm_sem.at[k, 1, off],
-                device_id={axis: lax.rem(me + off, count)}, device_id_type=MESH,
-            )
-            for off in range(1, count)
-        ]
-        for each in copies:
-            each.start()
-        for each in copies:
-            each.wait()
-        return sum(slots[i] for i in range(count))
-
-    norms[...] = jnp.zeros_like(norms)
-    for v in range(2):
-        for f in range(d.fields):
-            flat = sum(sums[v, f, :, k : k + LANES] for k in range(0, d.degrees, LANES))
-            norms[0, 4 * v + f : 4 * v + f + 1, :] = jnp.sum(flat, axis=0, keepdims=True)
-    norms[1] = spread("band", band, n, band_norms, 0)
-    total_out[...] = spread("node", node, d.nnode, node_norms, 1)
 
 
 def sweep(d, iterate, legendre, state, rate, trig, cor, weight, quadrature):

time: 263 us -> 260 us (0.989)
  Pallas kernels: 251 us -> 248 us
    pallas_call x1, Pallas kernels: 251 us -> 248 us  [sweep(): pl.pallas_call(functools.partial(sweep_kernel, d), name='sweep', out_shap...]
where the time goes in v4:
time: 260 us; the launch traced here: 259 us
  Pallas kernels  248 us (95%)
  local copies, waits for them, and re-layouts  8.49 us (3%)
    pallas_call x1, Pallas kernels, sweep(): pl.pallas_call(functools.partial(sweep_kernel, d), name='sweep', out_shap...  248 us
    unnamed x3, local copies, waits for them, and re-layouts  6.57 us

profile of v4, /device:TPU:0, one launch (start us, length us, event | category | flops | bytes accessed | tf_op | source)
XLA Modules:
  0.0 258.6 jit_solution(769440482848889515)
XLA Ops:
  0.6 0.0 copy-start
  0.7 0.8 dynamic_slice.7
  1.4 0.0 copy-done
  1.4 0.6 constant_dynamic-slice_fusion.cor
  2.0 0.6 tile.2
  2.6 248.1 %sweep.1 = (f32[1,2,128,3,4,512]{5,4,3,2,1,0:T(4,128)}, f32[8,128]{1,0:T(8,128)}, bf16[24,8,64,256]{3,2,1,0:T(8,128)(2,1)}, bf16[2,8,12,64,256]{4,3,2,1,0:T(8,128)(2,1)}) custom-call(f32[1,2,128,3,4,512]{5,4,3,2,1,0:T(4,128)} %bitcast.8, bf16[128,512,512]{2,1,0:T(8,128)(2,1)} %leg_hbm.1, f32[2,128,3,4,512]{4,3,2,1,0:T(4,128)} %bitcast.9, ...), custom_call_target="tpu_custom_call" | custom-call | tf_op jit(solution)/shard_map/sweep/pallas_call | solution.py:867
  250.7 0.8 slice_reduce_fusion
  251.5 0.5 sqrt_bitcast_fusion
  252.0 6.6 %copy.11 = f32[1,2,128,4,3,512]{5,3,4,2,1,0:T(4,128)} copy(f32[1,2,128,4,3,512]{5,3,4,2,1,0:T(4,128)} %bitcast.10) | data formatting | bytes 12582912
Async XLA Ops:
  0.6 0.8 copy-start
